TPU v7x, 256 devices: a whole 4x4x8 slice. The times are simulated.
256 devices in a mesh: ew: 16 (over x_hi, z), ns: 16 (over y, x_lo, core).
Axes of the slice: x: 4 (x_hi: 2, x_lo: 2; x = x_hi * 2 + x_lo), y: 4, z: 8, core: 2. Of those that a mesh axis runs over, the one named last changes fastest.
Arguments:
- temp: float32 [32, 256, 2048], P(None, 'ns', 'ew'), may hold values from -6 to 6
- salt: float32 [32, 256, 2048], P(None, 'ns', 'ew'), may hold values from -6 to 6
- u_east: float32 [32, 256, 2048], P(None, 'ns', 'ew'), may hold values from -0.25 to 0.25
- v_north: float32 [32, 256, 2048], P(None, 'ns', 'ew'), may hold values from -0.25 to 0.25
- wet: int32 [32, 256, 2048], P(None, 'ns', 'ew'), may hold values 0 or 1
- cot_temp: float32 [32, 256, 2048], P(None, 'ns', 'ew'), may hold values from -6 to 6
- cot_salt: float32 [32, 256, 2048], P(None, 'ns', 'ew'), may hold values from -6 to 6
Outputs:
- temp_final: float32 [32, 256, 2048], P(None, 'ns', 'ew')
- salt_final: float32 [32, 256, 2048], P(None, 'ns', 'ew')
- grad_temp: float32 [32, 256, 2048], P(None, 'ns', 'ew')
- grad_salt: float32 [32, 256, 2048], P(None, 'ns', 'ew')
All inputs are finite; a program needn't handle non-finite values. No bound on the sum of `wet` on one device may be relied on, other than what follows from the above.
Results may differ from a plain program's by a relative error of at most 0.00002.
Values sent between devices are 32-bit elements; how exact they have to be, the bound alone decides.
A program may use at most 64 MiB of HBM per device.

v0:
```python
import jax
import jax.numpy as jnp
from jax import lax
from jax.sharding import PartitionSpec as P

horizontal_mix = 0.05
vertical_mix = 0.2


def padded_2(cells, sides, width, closed):
    for axis, dim in sides:
        count = lax.axis_size(axis)
        ends = count if closed else count - 1
        head = lax.slice_in_dim(cells, 0, width, axis=dim)
        tail = lax.slice_in_dim(cells, cells.shape[dim] - width, cells.shape[dim], axis=dim)
        cells = jnp.concatenate(
            [
                lax.ppermute(tail, axis, [(i, (i + 1) % count) for i in range(ends)]),
                cells,
                lax.ppermute(head, axis, [((i + 1) % count, i) for i in range(ends)]),
            ],
            axis=dim,
        )
    return cells


def window_of(array, start, stop, axis):
    return lax.slice_in_dim(array, start, array.shape[axis] + stop, 1, axis)


def coefficients(speed):
    magnitude = jnp.abs(speed)
    return (
        (-speed - magnitude) / 12.0,
        (7.0 * speed + 3.0 * magnitude) / 12.0 + horizontal_mix,
        (7.0 * speed - 3.0 * magnitude) / 12.0 - horizontal_mix,
        (-speed + magnitude) / 12.0,
    )


def face_change(field, speed, wetness, axis):
    far_left = window_of(field, 0, -3, axis)
    left = window_of(field, 1, -2, axis)
    right = window_of(field, 2, -1, axis)
    far_right = window_of(field, 3, 0, axis)
    weights = coefficients(window_of(speed, 1, -2, axis))
    open_face = window_of(wetness, 1, -2, axis) * window_of(wetness, 2, -1, axis)
    flux = open_face * (
        weights[0] * far_left + weights[1] * left + weights[2] * right + weights[3] * far_right
    )
    return window_of(flux, 0, -1, axis) - window_of(flux, 1, 0, axis)


def face_adjoint(field, speed, wetness, axis):
    weighted = wetness * field
    jump = window_of(weighted, 1, 0, axis) - window_of(weighted, 0, -1, axis)
    open_face = window_of(wetness, 0, -1, axis) * window_of(wetness, 1, 0, axis)
    weights = coefficients(window_of(speed, 0, -1, axis))
    scaled = open_face * jump
    return (
        window_of(weights[0] * scaled, 3, 0, axis)
        + window_of(weights[1] * scaled, 2, -1, axis)
        + window_of(weights[2] * scaled, 1, -2, axis)
        + window_of(weights[3] * scaled, 0, -3, axis)
    )


def vertical_change(field, wetness):
    open_face = wetness[:, :-1] * wetness[:, 1:]
    flux = vertical_mix * open_face * (field[:, :-1] - field[:, 1:])
    return jnp.pad(flux, ((0, 0), (1, 0), (0, 0), (0, 0))) - jnp.pad(
        flux, ((0, 0), (0, 1), (0, 0), (0, 0))
    )


def vertical_adjoint(field, wetness):
    weighted = wetness * field
    open_face = wetness[:, :-1] * wetness[:, 1:]
    flux = vertical_mix * open_face * (weighted[:, 1:] - weighted[:, :-1])
    return jnp.pad(flux, ((0, 0), (0, 1), (0, 0), (0, 0))) - jnp.pad(
        flux, ((0, 0), (1, 0), (0, 0), (0, 0))
    )


def advance(padded, flow_wide):
    east_speed = flow_wide[0:1]
    north_speed = flow_wide[1:2]
    wetness = flow_wide[2:3]
    change_x = face_change(
        window_of(padded, 2, -2, 2),
        window_of(east_speed, 2, -2, 2),
        window_of(wetness, 2, -2, 2),
        3,
    )
    change_y = face_change(
        window_of(padded, 2, -2, 3),
        window_of(north_speed, 2, -2, 3),
        window_of(wetness, 2, -2, 3),
        2,
    )
    inner = window_of(window_of(padded, 2, -2, 2), 2, -2, 3)
    inner_wet = window_of(window_of(wetness, 2, -2, 2), 2, -2, 3)
    change_z = vertical_change(inner, inner_wet)
    return inner + inner_wet * (change_x + change_y + change_z)


def retreat(padded, flow_wide):
    east_speed = flow_wide[0:1]
    north_speed = flow_wide[1:2]
    wetness = flow_wide[2:3]
    back_x = face_adjoint(
        window_of(padded, 2, -2, 2),
        window_of(east_speed, 2, -2, 2),
        window_of(wetness, 2, -2, 2),
        3,
    )
    back_y = face_adjoint(
        window_of(padded, 2, -2, 3),
        window_of(north_speed, 2, -2, 3),
        window_of(wetness, 2, -2, 3),
        2,
    )
    inner = window_of(window_of(padded, 2, -2, 2), 2, -2, 3)
    inner_wet = window_of(window_of(wetness, 2, -2, 2), 2, -2, 3)
    back_z = vertical_adjoint(inner, inner_wet)
    return inner + back_x + back_y + back_z


def widen_state(field, width):
    across = padded_2(field, (("ew", 3),), width, True)
    return padded_2(across, (("ns", 2),), width, False)


def widen_flow(field, width):
    across = padded_2(field, (("ew", 3),), width, True)
    return padded_2(across, (("ns", 2),), width, False)


def evolve(field, flow_wide, stepper):
    for turn in range(2):
        field = stepper(widen_state(field, 2), flow_wide)
    return field


def local(temp, salt, u_east, v_north, wet, cot_temp, cot_salt):
    reach = 2
    flow_wide = widen_flow(jnp.stack([u_east, v_north, wet.astype(jnp.float32)]), reach)
    tracers = evolve(jnp.stack([temp, salt]), flow_wide, advance)
    sensitivity = evolve(jnp.stack([cot_temp, cot_salt]), flow_wide, retreat)
    return (tracers[0], tracers[1], sensitivity[0], sensitivity[1])


def solution(mesh):
    in_specs = (
        P(None, "ns", "ew"),
        P(None, "ns", "ew"),
        P(None, "ns", "ew"),
        P(None, "ns", "ew"),
        P(None, "ns", "ew"),
        P(None, "ns", "ew"),
        P(None, "ns", "ew"),
    )
    out_specs = (P(None, "ns", "ew"), P(None, "ns", "ew"), P(None, "ns", "ew"), P(None, "ns", "ew"))
    return jax.shard_map(local, mesh=mesh, in_specs=in_specs, out_specs=out_specs, check_vma=False)
```

profile of v0, /device:TPU:11, one launch (start us, length us, event | category | flops | bytes accessed | tf_op | source)
XLA Modules:
  0.0 143.5 jit_solution(3449930399045641063)
XLA Ops:
  7.4 5.5 %collective-permute-start.1 = (f32[3,32,16,2]{1,2,3,0:T(8,128)}, f32[3,32,16,2]{1,2,3,0:T(8,128)}, u32[]{:S(2)}, u32[]{:S(2)}) collective-permute-start(f32[3,32,16,2]{1,2,3,0:T(8,128)} %copy.87), channel_id=1, source_target_pairs={{16,0},{32,16},{48,32},{64,48},{80,64},{96,80},{112,96},{128,112},... | collective-permute-start | bytes 36872 | tf_op jit(solution)/shard_map/ppermute | solution.py:20
  14.3 5.1 %collective-permute-start.3 = (f32[2,32,16,2]{3,2,1,0:T(8,128)S(1)}, f32[2,32,16,2]{3,2,1,0:T(8,128)S(1)}, u32[]{:S(2)}, u32[]{:S(2)}) collective-permute-start(f32[2,32,16,2]{3,2,1,0:T(8,128)S(1)} %get-tuple-element.63), channel_id=1, source_target_pairs={{16,0},{32,16},{48,32},{64,48},{80,64},{96,80},{112,96},{128,112},... | collective-permute-start | bytes 24584 | tf_op jit(solution)/shard_map/ppermute | solution.py:20
  20.4 21.2 %collective-permute-done.2 = f32[2,32,16,2]{3,2,1,0:T(8,128)S(1)} collective-permute-done((f32[2,32,16,2]{3,2,1,0:T(8,128)S(1)}, f32[2,32,16,2]{3,2,1,0:T(8,128)S(1)}, u32[]{:S(2)}, u32[]{:S(2)}) %collective-permute-start.2) | collective-permute-done | bytes 8224 | tf_op jit(solution)/shard_map/ppermute | solution.py:18
  42.7 5.8 %collective-permute-start.6 = (f32[2,32,2,132]{3,2,1,0:T(2,128)}, f32[2,32,2,132]{3,2,1,0:T(2,128)}, u32[]{:S(2)}, u32[]{:S(2)}) collective-permute-start(f32[2,32,2,132]{3,2,1,0:T(2,128)} %get-tuple-element.39), channel_id=1, source_target_pairs={{0,1},{1,2},{2,3},{3,4},{4,5},{5,6},{6,7},{7,8},{8,9},{9,10},{10,1... | collective-permute-start | bytes 202760 | tf_op jit(solution)/shard_map/ppermute | solution.py:18
  48.9 1.9 %collective-permute-start.7 = (f32[2,32,2,132]{3,2,1,0:T(2,128)S(1)}, f32[2,32,2,132]{3,2,1,0:T(2,128)}, u32[]{:S(2)}, u32[]{:S(2)}) collective-permute-start(f32[2,32,2,132]{3,2,1,0:T(2,128)S(1)} %get-tuple-element.40), channel_id=1, source_target_pairs={{1,0},{2,1},{3,2},{4,3},{5,4},{6,5},{7,6},{8,7},{9,8},{10,9},{11,1... | collective-permute-start | bytes 202760 | tf_op jit(solution)/shard_map/ppermute | solution.py:20
  50.9 2.1 %copy.63 = f32[3,32,16,2]{3,2,1,0:T(8,128)} copy(f32[3,32,16,2]{1,2,3,0:T(8,128)} %collective-permute-done) | data formatting | bytes 24576 | tf_op jit(solution)/shard_map/ppermute | solution.py:18
  53.0 2.0 %copy.65 = f32[3,32,16,2]{3,2,1,0:T(8,128)} copy(f32[3,32,16,2]{1,2,3,0:T(8,128)} %collective-permute-done.1) | data formatting | bytes 24576 | tf_op jit(solution)/shard_map/ppermute | solution.py:20
  55.0 2.2 %pad_maximum_fusion = f32[3,32,16,132]{3,2,1,0:T(8,128)S(1)} fusion(f32[3,32,16,2]{3,2,1,0:T(8,128)} %copy.65, f32[1,32,16,128]{3,2,1,0:T(8,128)S(1)} %get-tuple-element.67, f32[1,32,16,128]{3,2,1,0:T(8,128)} %bitcast.85, f32[1,32,16,128]{3,2,1,0:T(8,128)} %bitcast.88, f32[3,32,16,2]{3,2,1,0:T(8,128)} %copy.63), kind=kLoop, calls=%fused_computation | loop fusion | flops 811008 | bytes 1622016 | tf_op jit(solution)/shard_map/concatenate | solution.py:16
  59.4 4.5 %collective-permute-start.4 = (f32[3,32,2,132]{3,2,1,0:T(2,128)S(1)}, f32[3,32,2,132]{3,2,1,0:T(2,128)S(1)}, u32[]{:S(2)}, u32[]{:S(2)}) collective-permute-start(f32[3,32,2,132]{3,2,1,0:T(2,128)S(1)} %get-tuple-element.36), channel_id=1, source_target_pairs={{0,1},{1,2},{2,3},{3,4},{4,5},{5,6},{6,7},{7,8},{8,9},{9,10},{10,1... | collective-permute-start | bytes 304136 | tf_op jit(solution)/shard_map/ppermute | solution.py:18
  64.0 1.9 %collective-permute-start.5 = (f32[3,32,2,132]{3,2,1,0:T(2,128)S(1)}, f32[3,32,2,132]{3,2,1,0:T(2,128)S(1)}, u32[]{:S(2)}, u32[]{:S(2)}) collective-permute-start(f32[3,32,2,132]{3,2,1,0:T(2,128)S(1)} %get-tuple-element.35), channel_id=1, source_target_pairs={{1,0},{2,1},{3,2},{4,3},{5,4},{6,5},{7,6},{8,7},{9,8},{10,9},{11,1... | collective-permute-start | bytes 304136 | tf_op jit(solution)/shard_map/ppermute | solution.py:20
  67.7 4.5 %collective-permute-start.14 = (f32[2,32,2,132]{3,2,1,0:T(2,128)S(1)}, f32[2,32,2,132]{3,2,1,0:T(2,128)S(1)}, u32[]{:S(2)}, u32[]{:S(2)}) collective-permute-start(f32[2,32,2,132]{3,2,1,0:T(2,128)S(1)} %get-tuple-element.43), channel_id=1, source_target_pairs={{0,1},{1,2},{2,3},{3,4},{4,5},{5,6},{6,7},{7,8},{8,9},{9,10},{10,1... | collective-permute-start | bytes 202760 | tf_op jit(solution)/shard_map/ppermute | solution.py:18
  74.2 2.1 %collective-permute-start.15 = (f32[2,32,2,132]{3,2,1,0:T(2,128)S(1)}, f32[2,32,2,132]{3,2,1,0:T(2,128)S(1)}, u32[]{:S(2)}, u32[]{:S(2)}) collective-permute-start(f32[2,32,2,132]{3,2,1,0:T(2,128)S(1)} %get-tuple-element.44), channel_id=1, source_target_pairs={{1,0},{2,1},{3,2},{4,3},{5,4},{6,5},{7,6},{8,7},{9,8},{10,9},{11,1... | collective-permute-start | bytes 202760 | tf_op jit(solution)/shard_map/ppermute | solution.py:20
  76.4 2.1 %maximum_maximum_fusion = (f32[2,32,18,132]{3,2,1,0:T(8,128)S(1)}, f32[2,32,18,132]{3,2,1,0:T(8,128)S(1)}) fusion(f32[2,32,16,2]{3,2,1,0:T(8,128)S(1)} %copy-done.11, f32[1,32,16,128]{3,2,1,0:T(8,128)S(1)} %bitcast.66, f32[1,32,16,128]{3,2,1,0:T(8,128)S(1)} %bitcast.72, f32[2,32,16,2]{3,2,1,0:T(8,128)S(1)} %copy-done.9, ...), kind=kLoop, calls=%fused_computation.1 | loop fusion | flops 1216512 | bytes 1892352 | tf_op jit(solution)/shard_map/concatenate | solution.py:16
  83.3 1.8 %collective-permute-start.8 = (f32[2,32,16,2]{3,2,1,0:T(8,128)S(1)}, f32[2,32,16,2]{3,2,1,0:T(8,128)S(1)}, u32[]{:S(2)}, u32[]{:S(2)}) collective-permute-start(f32[2,32,16,2]{3,2,1,0:T(8,128)S(1)} %get-tuple-element.55), channel_id=1, source_target_pairs={{0,16},{16,32},{32,48},{48,64},{64,80},{80,96},{96,112},{112,128},... | collective-permute-start | bytes 24584 | tf_op jit(solution)/shard_map/ppermute | solution.py:18
  85.1 3.3 %collective-permute-start.9 = (f32[2,32,16,2]{3,2,1,0:T(8,128)S(1)}, f32[2,32,16,2]{3,2,1,0:T(8,128)S(1)}, u32[]{:S(2)}, u32[]{:S(2)}) collective-permute-start(f32[2,32,16,2]{3,2,1,0:T(8,128)S(1)} %get-tuple-element.56), channel_id=1, source_target_pairs={{16,0},{32,16},{48,32},{64,48},{80,64},{96,80},{112,96},{128,112},... | collective-permute-start | bytes 24584 | tf_op jit(solution)/shard_map/ppermute | solution.py:20
  91.7 7.3 %collective-permute-done.8 = f32[2,32,16,2]{3,2,1,0:T(8,128)S(1)} collective-permute-done((f32[2,32,16,2]{3,2,1,0:T(8,128)S(1)}, f32[2,32,16,2]{3,2,1,0:T(8,128)S(1)}, u32[]{:S(2)}, u32[]{:S(2)}) %collective-permute-start.8) | collective-permute-done | bytes 8224 | tf_op jit(solution)/shard_map/ppermute | solution.py:18
  99.5 4.3 %collective-permute-start.10 = (f32[2,32,2,132]{3,2,1,0:T(2,128)S(1)}, f32[2,32,2,132]{3,2,1,0:T(2,128)S(1)}, u32[]{:S(2)}, u32[]{:S(2)}) collective-permute-start(f32[2,32,2,132]{3,2,1,0:T(2,128)S(1)} %get-tuple-element.32), channel_id=1, source_target_pairs={{0,1},{1,2},{2,3},{3,4},{4,5},{5,6},{6,7},{7,8},{8,9},{9,10},{10,1... | collective-permute-start | bytes 202760 | tf_op jit(solution)/shard_map/ppermute | solution.py:18
  103.7 2.1 %collective-permute-start.11 = (f32[2,32,2,132]{3,2,1,0:T(2,128)S(1)}, f32[2,32,2,132]{3,2,1,0:T(2,128)S(1)}, u32[]{:S(2)}, u32[]{:S(2)}) collective-permute-start(f32[2,32,2,132]{3,2,1,0:T(2,128)S(1)} %get-tuple-element.33), channel_id=1, source_target_pairs={{1,0},{2,1},{3,2},{4,3},{5,4},{6,5},{7,6},{8,7},{9,8},{10,9},{11,1... | collective-permute-start | bytes 202760 | tf_op jit(solution)/shard_map/ppermute | solution.py:20
  107.1 3.9 %collective-permute-done.11 = f32[2,32,2,132]{3,2,1,0:T(2,128)S(1)} collective-permute-done((f32[2,32,2,132]{3,2,1,0:T(2,128)S(1)}, f32[2,32,2,132]{3,2,1,0:T(2,128)S(1)}, u32[]{:S(2)}, u32[]{:S(2)}) %collective-permute-start.11) | collective-permute-done | bytes 67616 | tf_op jit(solution)/shard_map/ppermute | solution.py:20
  114.2 5.1 %collective-permute-start.17 = (f32[2,32,16,2]{3,2,1,0:T(8,128)S(1)}, f32[2,32,16,2]{3,2,1,0:T(8,128)S(1)}, u32[]{:S(2)}, u32[]{:S(2)}) collective-permute-start(f32[2,32,16,2]{3,2,1,0:T(8,128)S(1)} %get-tuple-element.50), channel_id=1, source_target_pairs={{16,0},{32,16},{48,32},{64,48},{80,64},{96,80},{112,96},{128,112},... | collective-permute-start | bytes 24584 | tf_op jit(solution)/shard_map/ppermute | solution.py:20
  119.4 9.1 %collective-permute-done.16 = f32[2,32,16,2]{3,2,1,0:T(8,128)S(1)} collective-permute-done((f32[2,32,16,2]{3,2,1,0:T(8,128)S(1)}, f32[2,32,16,2]{3,2,1,0:T(8,128)S(1)}, u32[]{:S(2)}, u32[]{:S(2)}) %collective-permute-start.16) | collective-permute-done | bytes 8224 | tf_op jit(solution)/shard_map/ppermute | solution.py:18
  129.1 5.1 %collective-permute-start.18 = (f32[2,32,2,132]{3,2,1,0:T(2,128)S(1)}, f32[2,32,2,132]{3,2,1,0:T(2,128)S(1)}, u32[]{:S(2)}, u32[]{:S(2)}) collective-permute-start(f32[2,32,2,132]{3,2,1,0:T(2,128)S(1)} %get-tuple-element.41), channel_id=1, source_target_pairs={{0,1},{1,2},{2,3},{3,4},{4,5},{5,6},{6,7},{7,8},{8,9},{9,10},{10,1... | collective-permute-start | bytes 202760 | tf_op jit(solution)/shard_map/ppermute | solution.py:18
  134.2 1.9 %collective-permute-start.19 = (f32[2,32,2,132]{3,2,1,0:T(2,128)S(1)}, f32[2,32,2,132]{3,2,1,0:T(2,128)S(1)}, u32[]{:S(2)}, u32[]{:S(2)}) collective-permute-start(f32[2,32,2,132]{3,2,1,0:T(2,128)S(1)} %get-tuple-element.42), channel_id=1, source_target_pairs={{1,0},{2,1},{3,2},{4,3},{5,4},{6,5},{7,6},{8,7},{9,8},{10,9},{11,1... | collective-permute-start | bytes 202760 | tf_op jit(solution)/shard_map/ppermute | solution.py:20
  137.2 4.2 %collective-permute-done.19 = f32[2,32,2,132]{3,2,1,0:T(2,128)S(1)} collective-permute-done((f32[2,32,2,132]{3,2,1,0:T(2,128)S(1)}, f32[2,32,2,132]{3,2,1,0:T(2,128)S(1)}, u32[]{:S(2)}, u32[]{:S(2)}) %collective-permute-start.19) | collective-permute-done | bytes 67616 | tf_op jit(solution)/shard_map/ppermute | solution.py:20
  (119 shorter events, 33.1 us)
Async XLA Ops:
  3.7 9.2 %copy-start.4 = (f32[32,16,128]{2,1,0:T(8,128)S(1)}, f32[32,16,128]{2,1,0:T(8,128)}, u32[]{:S(2)}) copy-start(f32[32,16,128]{2,1,0:T(8,128)} %param.13) | copy-start | bytes 786436
  3.7 10.3 %copy-start = (f32[32,16,128]{2,1,0:T(8,128)S(1)}, f32[32,16,128]{2,1,0:T(8,128)}, u32[]{:S(2)}) copy-start(f32[32,16,128]{2,1,0:T(8,128)} %param.8) | copy-start | bytes 786436
  3.7 10.3 %copy-start.1 = (f32[32,16,128]{2,1,0:T(8,128)S(1)}, f32[32,16,128]{2,1,0:T(8,128)}, u32[]{:S(2)}) copy-start(f32[32,16,128]{2,1,0:T(8,128)} %param.7) | copy-start | bytes 786436
  4.7 44.2 %collective-permute-start = (f32[3,32,16,2]{1,2,3,0:T(8,128)}, f32[3,32,16,2]{1,2,3,0:T(8,128)}, u32[]{:S(2)}, u32[]{:S(2)}) collective-permute-start(f32[3,32,16,2]{1,2,3,0:T(8,128)} %copy.86), channel_id=1, source_target_pairs={{0,16},{16,32},{32,48},{48,64},{64,80},{80,96},{96,112},{112,128},... | collective-permute-start | bytes 36872 | tf_op jit(solution)/shard_map/ppermute | solution.py:18
  7.4 45.6 %collective-permute-start.1 = (f32[3,32,16,2]{1,2,3,0:T(8,128)}, f32[3,32,16,2]{1,2,3,0:T(8,128)}, u32[]{:S(2)}, u32[]{:S(2)}) collective-permute-start(f32[3,32,16,2]{1,2,3,0:T(8,128)} %copy.87), channel_id=1, source_target_pairs={{16,0},{32,16},{48,32},{64,48},{80,64},{96,80},{112,96},{128,112},... | collective-permute-start | bytes 36872 | tf_op jit(solution)/shard_map/ppermute | solution.py:20
  14.0 49.9 %collective-permute-start.12 = (f32[2,32,16,2]{3,2,1,0:T(8,128)}, f32[2,32,16,2]{3,2,1,0:T(8,128)}, u32[]{:S(2)}, u32[]{:S(2)}) collective-permute-start(f32[2,32,16,2]{3,2,1,0:T(8,128)} %get-tuple-element.51), channel_id=1, source_target_pairs={{0,16},{16,32},{32,48},{48,64},{64,80},{80,96},{96,112},{112,128},... | collective-permute-start | bytes 24584 | tf_op jit(solution)/shard_map/ppermute | solution.py:18
  14.2 27.3 %collective-permute-start.2 = (f32[2,32,16,2]{3,2,1,0:T(8,128)S(1)}, f32[2,32,16,2]{3,2,1,0:T(8,128)S(1)}, u32[]{:S(2)}, u32[]{:S(2)}) collective-permute-start(f32[2,32,16,2]{3,2,1,0:T(8,128)S(1)} %get-tuple-element.62), channel_id=1, source_target_pairs={{0,16},{16,32},{32,48},{48,64},{64,80},{80,96},{96,112},{112,128},... | collective-permute-start | bytes 24584 | tf_op jit(solution)/shard_map/ppermute | solution.py:18
  14.3 27.2 %collective-permute-start.3 = (f32[2,32,16,2]{3,2,1,0:T(8,128)S(1)}, f32[2,32,16,2]{3,2,1,0:T(8,128)S(1)}, u32[]{:S(2)}, u32[]{:S(2)}) collective-permute-start(f32[2,32,16,2]{3,2,1,0:T(8,128)S(1)} %get-tuple-element.63), channel_id=1, source_target_pairs={{16,0},{32,16},{48,32},{64,48},{80,64},{96,80},{112,96},{128,112},... | collective-permute-start | bytes 24584 | tf_op jit(solution)/shard_map/ppermute | solution.py:20
  19.5 23.2 %copy-start.6 = (f32[31,16,128]{2,1,0:T(8,128)}, f32[31,16,128]{2,1,0:T(8,128)S(1)}, u32[]{:S(2)}) copy-start(f32[31,16,128]{2,1,0:T(8,128)S(1)} %fusion.69) | copy-start | bytes 761860
  41.6 24.3 %collective-permute-start.13 = (f32[2,32,16,2]{3,2,1,0:T(8,128)}, f32[2,32,16,2]{3,2,1,0:T(8,128)}, u32[]{:S(2)}, u32[]{:S(2)}) collective-permute-start(f32[2,32,16,2]{3,2,1,0:T(8,128)} %get-tuple-element.52), channel_id=1, source_target_pairs={{16,0},{32,16},{48,32},{64,48},{80,64},{96,80},{112,96},{128,112},... | collective-permute-start | bytes 24584 | tf_op jit(solution)/shard_map/ppermute | solution.py:20
  42.7 31.5 %collective-permute-start.6 = (f32[2,32,2,132]{3,2,1,0:T(2,128)}, f32[2,32,2,132]{3,2,1,0:T(2,128)}, u32[]{:S(2)}, u32[]{:S(2)}) collective-permute-start(f32[2,32,2,132]{3,2,1,0:T(2,128)} %get-tuple-element.39), channel_id=1, source_target_pairs={{0,1},{1,2},{2,3},{3,4},{4,5},{5,6},{6,7},{7,8},{8,9},{9,10},{10,1... | collective-permute-start | bytes 202760 | tf_op jit(solution)/shard_map/ppermute | solution.py:18
  48.9 27.4 %collective-permute-start.7 = (f32[2,32,2,132]{3,2,1,0:T(2,128)S(1)}, f32[2,32,2,132]{3,2,1,0:T(2,128)}, u32[]{:S(2)}, u32[]{:S(2)}) collective-permute-start(f32[2,32,2,132]{3,2,1,0:T(2,128)S(1)} %get-tuple-element.40), channel_id=1, source_target_pairs={{1,0},{2,1},{3,2},{4,3},{5,4},{6,5},{7,6},{8,7},{9,8},{10,9},{11,1... | collective-permute-start | bytes 202760 | tf_op jit(solution)/shard_map/ppermute | solution.py:20
  59.4 19.0 %collective-permute-start.4 = (f32[3,32,2,132]{3,2,1,0:T(2,128)S(1)}, f32[3,32,2,132]{3,2,1,0:T(2,128)S(1)}, u32[]{:S(2)}, u32[]{:S(2)}) collective-permute-start(f32[3,32,2,132]{3,2,1,0:T(2,128)S(1)} %get-tuple-element.36), channel_id=1, source_target_pairs={{0,1},{1,2},{2,3},{3,4},{4,5},{5,6},{6,7},{7,8},{8,9},{9,10},{10,1... | collective-permute-start | bytes 304136 | tf_op jit(solution)/shard_map/ppermute | solution.py:18
  64.0 15.5 %collective-permute-start.5 = (f32[3,32,2,132]{3,2,1,0:T(2,128)S(1)}, f32[3,32,2,132]{3,2,1,0:T(2,128)S(1)}, u32[]{:S(2)}, u32[]{:S(2)}) collective-permute-start(f32[3,32,2,132]{3,2,1,0:T(2,128)S(1)} %get-tuple-element.35), channel_id=1, source_target_pairs={{1,0},{2,1},{3,2},{4,3},{5,4},{6,5},{7,6},{8,7},{9,8},{10,9},{11,1... | collective-permute-start | bytes 304136 | tf_op jit(solution)/shard_map/ppermute | solution.py:20
  67.7 20.8 %collective-permute-start.14 = (f32[2,32,2,132]{3,2,1,0:T(2,128)S(1)}, f32[2,32,2,132]{3,2,1,0:T(2,128)S(1)}, u32[]{:S(2)}, u32[]{:S(2)}) collective-permute-start(f32[2,32,2,132]{3,2,1,0:T(2,128)S(1)} %get-tuple-element.43), channel_id=1, source_target_pairs={{0,1},{1,2},{2,3},{3,4},{4,5},{5,6},{6,7},{7,8},{8,9},{9,10},{10,1... | collective-permute-start | bytes 202760 | tf_op jit(solution)/shard_map/ppermute | solution.py:18
  74.2 14.3 %collective-permute-start.15 = (f32[2,32,2,132]{3,2,1,0:T(2,128)S(1)}, f32[2,32,2,132]{3,2,1,0:T(2,128)S(1)}, u32[]{:S(2)}, u32[]{:S(2)}) collective-permute-start(f32[2,32,2,132]{3,2,1,0:T(2,128)S(1)} %get-tuple-element.44), channel_id=1, source_target_pairs={{1,0},{2,1},{3,2},{4,3},{5,4},{6,5},{7,6},{8,7},{9,8},{10,9},{11,1... | collective-permute-start | bytes 202760 | tf_op jit(solution)/shard_map/ppermute | solution.py:20
  83.3 15.7 %collective-permute-start.8 = (f32[2,32,16,2]{3,2,1,0:T(8,128)S(1)}, f32[2,32,16,2]{3,2,1,0:T(8,128)S(1)}, u32[]{:S(2)}, u32[]{:S(2)}) collective-permute-start(f32[2,32,16,2]{3,2,1,0:T(8,128)S(1)} %get-tuple-element.55), channel_id=1, source_target_pairs={{0,16},{16,32},{32,48},{48,64},{64,80},{80,96},{96,112},{112,128},... | collective-permute-start | bytes 24584 | tf_op jit(solution)/shard_map/ppermute | solution.py:18
  85.1 13.9 %collective-permute-start.9 = (f32[2,32,16,2]{3,2,1,0:T(8,128)S(1)}, f32[2,32,16,2]{3,2,1,0:T(8,128)S(1)}, u32[]{:S(2)}, u32[]{:S(2)}) collective-permute-start(f32[2,32,16,2]{3,2,1,0:T(8,128)S(1)} %get-tuple-element.56), channel_id=1, source_target_pairs={{16,0},{32,16},{48,32},{64,48},{80,64},{96,80},{112,96},{128,112},... | collective-permute-start | bytes 24584 | tf_op jit(solution)/shard_map/ppermute | solution.py:20
  99.5 7.6 %collective-permute-start.10 = (f32[2,32,2,132]{3,2,1,0:T(2,128)S(1)}, f32[2,32,2,132]{3,2,1,0:T(2,128)S(1)}, u32[]{:S(2)}, u32[]{:S(2)}) collective-permute-start(f32[2,32,2,132]{3,2,1,0:T(2,128)S(1)} %get-tuple-element.32), channel_id=1, source_target_pairs={{0,1},{1,2},{2,3},{3,4},{4,5},{5,6},{6,7},{7,8},{8,9},{9,10},{10,1... | collective-permute-start | bytes 202760 | tf_op jit(solution)/shard_map/ppermute | solution.py:18
  103.7 7.2 %collective-permute-start.11 = (f32[2,32,2,132]{3,2,1,0:T(2,128)S(1)}, f32[2,32,2,132]{3,2,1,0:T(2,128)S(1)}, u32[]{:S(2)}, u32[]{:S(2)}) collective-permute-start(f32[2,32,2,132]{3,2,1,0:T(2,128)S(1)} %get-tuple-element.33), channel_id=1, source_target_pairs={{1,0},{2,1},{3,2},{4,3},{5,4},{6,5},{7,6},{8,7},{9,8},{10,9},{11,1... | collective-permute-start | bytes 202760 | tf_op jit(solution)/shard_map/ppermute | solution.py:20
  114.1 14.3 %collective-permute-start.16 = (f32[2,32,16,2]{3,2,1,0:T(8,128)S(1)}, f32[2,32,16,2]{3,2,1,0:T(8,128)S(1)}, u32[]{:S(2)}, u32[]{:S(2)}) collective-permute-start(f32[2,32,16,2]{3,2,1,0:T(8,128)S(1)} %get-tuple-element.49), channel_id=1, source_target_pairs={{0,16},{16,32},{32,48},{48,64},{64,80},{80,96},{96,112},{112,128},... | collective-permute-start | bytes 24584 | tf_op jit(solution)/shard_map/ppermute | solution.py:18
  114.2 14.2 %collective-permute-start.17 = (f32[2,32,16,2]{3,2,1,0:T(8,128)S(1)}, f32[2,32,16,2]{3,2,1,0:T(8,128)S(1)}, u32[]{:S(2)}, u32[]{:S(2)}) collective-permute-start(f32[2,32,16,2]{3,2,1,0:T(8,128)S(1)} %get-tuple-element.50), channel_id=1, source_target_pairs={{16,0},{32,16},{48,32},{64,48},{80,64},{96,80},{112,96},{128,112},... | collective-permute-start | bytes 24584 | tf_op jit(solution)/shard_map/ppermute | solution.py:20
  129.1 8.1 %collective-permute-start.18 = (f32[2,32,2,132]{3,2,1,0:T(2,128)S(1)}, f32[2,32,2,132]{3,2,1,0:T(2,128)S(1)}, u32[]{:S(2)}, u32[]{:S(2)}) collective-permute-start(f32[2,32,2,132]{3,2,1,0:T(2,128)S(1)} %get-tuple-element.41), channel_id=1, source_target_pairs={{0,1},{1,2},{2,3},{3,4},{4,5},{5,6},{6,7},{7,8},{8,9},{9,10},{10,1... | collective-permute-start | bytes 202760 | tf_op jit(solution)/shard_map/ppermute | solution.py:18
  134.2 7.2 %collective-permute-start.19 = (f32[2,32,2,132]{3,2,1,0:T(2,128)S(1)}, f32[2,32,2,132]{3,2,1,0:T(2,128)S(1)}, u32[]{:S(2)}, u32[]{:S(2)}) collective-permute-start(f32[2,32,2,132]{3,2,1,0:T(2,128)S(1)} %get-tuple-element.42), channel_id=1, source_target_pairs={{1,0},{2,1},{3,2},{4,3},{5,4},{6,5},{7,6},{8,7},{9,8},{10,9},{11,1... | collective-permute-start | bytes 202760 | tf_op jit(solution)/shard_map/ppermute | solution.py:20
  (12 other events, 37.5 us)
where the time goes:
time: 144 us
  starting transfers between devices  57 us (40%)
  waiting for transfers between devices  46.3 us (32%)
  other arithmetic  25.1 us (17%)
  local copies, waits for them, and re-layouts  13.9 us (10%)
    ppermute x10, waiting for transfers between devices, padded_2(): lax.ppermute(tail, axis, [(i, (i + 1) % count) for i in range(ends)])  38.2 us
    ppermute x10, starting transfers between devices, padded_2(): lax.ppermute(head, axis, [((i + 1) % count, i) for i in range(ends)])  29.1 us
    ppermute x10, starting transfers between devices, padded_2(): lax.ppermute(tail, axis, [(i, (i + 1) % count) for i in range(ends)])  27.9 us
    ppermute x10, waiting for transfers between devices, padded_2(): lax.ppermute(head, axis, [((i + 1) % count, i) for i in range(ends)])  8.09 us
    unnamed x40, local copies, waits for them, and re-layouts  5.81 us
    concatenate x4, other arithmetic, padded_2(): jnp.concatenate([lax.ppermute(tail, axis, [(i, (i + 1) % count) for i in...  5.74 us
    mul x5, other arithmetic, face_change(): open_face * (weights[0] * far_left + weights[1] * left + weights[2] * rig...  4.12 us
    mul x4, other arithmetic, face_adjoint(): weighted = wetness * field  4.1 us
  transfers between devices with their start and end apart: 20, of which 6 were waited for; matrix products, arithmetic and copies ran while one was open for 18% of the time, Pallas kernels for 0%

commit v1 on v0

v1 whole, which is shorter than its diff:
```python
import jax
import jax.numpy as jnp
from jax import lax
from jax.sharding import PartitionSpec as P

horizontal_mix = 0.05
vertical_mix = 0.2
HALO = 4


def window_of(array, start, stop, axis):
    return lax.slice_in_dim(array, start, array.shape[axis] + stop, 1, axis)


def coefficients(speed):
    magnitude = jnp.abs(speed)
    return (
        (-speed - magnitude) / 12.0,
        (7.0 * speed + 3.0 * magnitude) / 12.0 + horizontal_mix,
        (7.0 * speed - 3.0 * magnitude) / 12.0 - horizontal_mix,
        (-speed + magnitude) / 12.0,
    )


def face_change(field, speed, wetness, axis):
    far_left = window_of(field, 0, -3, axis)
    left = window_of(field, 1, -2, axis)
    right = window_of(field, 2, -1, axis)
    far_right = window_of(field, 3, 0, axis)
    weights = coefficients(window_of(speed, 1, -2, axis))
    open_face = window_of(wetness, 1, -2, axis) * window_of(wetness, 2, -1, axis)
    flux = open_face * (
        weights[0] * far_left + weights[1] * left + weights[2] * right + weights[3] * far_right
    )
    return window_of(flux, 0, -1, axis) - window_of(flux, 1, 0, axis)


def face_adjoint(field, speed, wetness, axis):
    weighted = wetness * field
    jump = window_of(weighted, 1, 0, axis) - window_of(weighted, 0, -1, axis)
    open_face = window_of(wetness, 0, -1, axis) * window_of(wetness, 1, 0, axis)
    weights = coefficients(window_of(speed, 0, -1, axis))
    scaled = open_face * jump
    return (
        window_of(weights[0] * scaled, 3, 0, axis)
        + window_of(weights[1] * scaled, 2, -1, axis)
        + window_of(weights[2] * scaled, 1, -2, axis)
        + window_of(weights[3] * scaled, 0, -3, axis)
    )


def vertical_change(field, wetness):
    open_face = wetness[:, :-1] * wetness[:, 1:]
    flux = vertical_mix * open_face * (field[:, :-1] - field[:, 1:])
    return jnp.pad(flux, ((0, 0), (1, 0), (0, 0), (0, 0))) - jnp.pad(
        flux, ((0, 0), (0, 1), (0, 0), (0, 0))
    )


def vertical_adjoint(field, wetness):
    weighted = wetness * field
    open_face = wetness[:, :-1] * wetness[:, 1:]
    flux = vertical_mix * open_face * (weighted[:, 1:] - weighted[:, :-1])
    return jnp.pad(flux, ((0, 0), (0, 1), (0, 0), (0, 0))) - jnp.pad(
        flux, ((0, 0), (1, 0), (0, 0), (0, 0))
    )


def split_flow(flow):
    return flow[0:1], flow[1:2], flow[2:3]


def advance(padded, flow):
    east_speed, north_speed, wetness = split_flow(flow)
    change_x = face_change(
        window_of(padded, 2, -2, 2), window_of(east_speed, 2, -2, 2), window_of(wetness, 2, -2, 2), 3
    )
    change_y = face_change(
        window_of(padded, 2, -2, 3), window_of(north_speed, 2, -2, 3), window_of(wetness, 2, -2, 3), 2
    )
    inner = window_of(window_of(padded, 2, -2, 2), 2, -2, 3)
    inner_wet = window_of(window_of(wetness, 2, -2, 2), 2, -2, 3)
    change_z = vertical_change(inner, inner_wet)
    return inner + inner_wet * (change_x + change_y + change_z)


def retreat(padded, flow):
    east_speed, north_speed, wetness = split_flow(flow)
    back_x = face_adjoint(
        window_of(padded, 2, -2, 2), window_of(east_speed, 2, -2, 2), window_of(wetness, 2, -2, 2), 3
    )
    back_y = face_adjoint(
        window_of(padded, 2, -2, 3), window_of(north_speed, 2, -2, 3), window_of(wetness, 2, -2, 3), 2
    )
    inner = window_of(window_of(padded, 2, -2, 2), 2, -2, 3)
    inner_wet = window_of(window_of(wetness, 2, -2, 2), 2, -2, 3)
    back_z = vertical_adjoint(inner, inner_wet)
    return inner + back_x + back_y + back_z


def with_halo(cells, width):
    n_ns = lax.axis_size("ns")
    n_ew = lax.axis_size("ew")
    axes = ("ew", "ns")

    def send(piece, d_ns, d_ew):
        pairs = []
        for a in range(n_ns):
            b = a + d_ns
            if b < 0 or b >= n_ns:
                continue
            for e in range(n_ew):
                f = (e + d_ew) % n_ew
                pairs.append((e * n_ns + a, f * n_ns + b))
        return lax.ppermute(piece, axes, pairs)

    rows, cols = cells.shape[-2], cells.shape[-1]
    lo_r, hi_r = slice(0, width), slice(rows - width, rows)
    lo_c, hi_c = slice(0, width), slice(cols - width, cols)
    every = slice(None)
    lead = (every,) * (cells.ndim - 2)

    def part(r, c):
        return cells[lead + (r, c)]

    south_west = send(part(hi_r, hi_c), 1, 1)
    south = send(part(hi_r, every), 1, 0)
    south_east = send(part(hi_r, lo_c), 1, -1)
    west = send(part(every, hi_c), 0, 1)
    east = send(part(every, lo_c), 0, -1)
    north_west = send(part(lo_r, hi_c), -1, 1)
    north = send(part(lo_r, every), -1, 0)
    north_east = send(part(lo_r, lo_c), -1, -1)
    bottom = jnp.concatenate([south_west, south, south_east], axis=-1)
    middle = jnp.concatenate([west, cells, east], axis=-1)
    top = jnp.concatenate([north_west, north, north_east], axis=-1)
    return jnp.concatenate([bottom, middle, top], axis=-2)


def local(temp, salt, u_east, v_north, wet, cot_temp, cot_salt):
    fields = jnp.stack(
        [temp, salt, cot_temp, cot_salt, u_east, v_north, wet.astype(jnp.float32)]
    )
    wide = with_halo(fields, HALO)
    tracers, flow = wide[0:2], wide[4:7]
    sens = wide[2:4]
    for turn in range(2):
        tracers = advance(tracers, flow)
        sens = retreat(sens, flow)
        flow = window_of(window_of(flow, 2, -2, 2), 2, -2, 3)
    return (tracers[0], tracers[1], sens[0], sens[1])


def solution(mesh):
    spec = P(None, "ns", "ew")
    return jax.shard_map(
        local, mesh=mesh, in_specs=(spec,) * 7, out_specs=(spec,) * 4, check_vma=False
    )
```

time: 144 us -> 125 us (0.87)
  the two profiles are of different devices: /device:TPU:11 before, /device:TPU:8 now
where the time goes in v1:
time: 125 us; the launch traced here: 123 us
  local copies, waits for them, and re-layouts  48.2 us (39%)
  other arithmetic  34.8 us (28%)
  starting transfers between devices  31.2 us (25%)
  waiting for transfers between devices  8.03 us (6%)
    ppermute x8, starting transfers between devices, send(): return lax.ppermute(piece, axes, pairs)  31.2 us
    unnamed x88, local copies, waits for them, and re-layouts  22 us
    ppermute x8, waiting for transfers between devices, send(): return lax.ppermute(piece, axes, pairs)  8.03 us
    mul x6, other arithmetic, face_change(): open_face * (weights[0] * far_left + weights[1] * left + weights[2] * rig...  6.49 us
    mul x4, other arithmetic, face_adjoint(): weights[0] * scaled  5.24 us
    slice x3, local copies, waits for them, and re-layouts, part(): return cells[lead + (r, c)]  5.18 us
    slice x14, local copies, waits for them, and re-layouts, window_of(): return lax.slice_in_dim(array, start, array.shape[axis] + stop, 1, axis)  4.59 us
    mul x4, local copies, waits for them, and re-layouts, face_adjoint(): weighted = wetness * field  4.06 us
  transfers between devices with their start and end apart: 8, of which 1 were waited for; matrix products, arithmetic and copies ran while one was open for 27% of the time, Pallas kernels for 0%

profile of v1, /device:TPU:8, one launch (start us, length us, event | category | flops | bytes accessed | tf_op | source)
XLA Modules:
  0.0 123.4 jit_solution(17502503269807960725)
XLA Ops:
  3.8 1.6 %fusion.64 = (f32[7,32,4,4]{3,2,1,0:T(4,128)S(1)}, f32[7,32,4,4]{3,2,1,0:T(4,128)}, f32[7,32,4,4]{3,2,1,0:T(4,128)S(1)}, f32[7,32,4,4]{3,2,1,0:T(4,128)}) fusion(f32[7,32,16,128]{3,2,1,0:T(8,128)S(1)} %constant_dynamic-update-slice_fusion), kind=kLoop, calls=%fused_computation.183 | loop fusion | bytes 114688 | tf_op jit(solution)/shard_map/slice | solution.py:124
  6.3 3.3 %collective-permute-start = (f32[7,32,4,4]{3,1,2,0:T(8,128)}, f32[7,32,4,4]{3,1,2,0:T(8,128)S(1)}, u32[]{:S(2)}, u32[]{:S(2)}) collective-permute-start(f32[7,32,4,4]{3,1,2,0:T(8,128)} %copy.64), channel_id=1, source_target_pairs={{0,17},{16,33},{32,49},{48,65},{64,81},{80,97},{96,113},{112,129},... | collective-permute-start | bytes 43016 | tf_op jit(solution)/shard_map/ppermute | solution.py:115
  10.4 8.3 %collective-permute-start.2 = (f32[7,32,4,4]{3,1,2,0:T(8,128)}, f32[7,32,4,4]{3,1,2,0:T(8,128)}, u32[]{:S(2)}, u32[]{:S(2)}) collective-permute-start(f32[7,32,4,4]{3,1,2,0:T(8,128)} %copy.66), channel_id=1, source_target_pairs={{0,241},{16,1},{32,17},{48,33},{64,49},{80,65},{96,81},{112,97},{1... | collective-permute-start | bytes 43016 | tf_op jit(solution)/shard_map/ppermute | solution.py:115
  20.5 2.3 %collective-permute-start.1 = (f32[7,32,4,128]{3,1,2,0:T(8,128)}, f32[7,32,4,128]{3,1,2,0:T(8,128)}, u32[]{:S(2)}, u32[]{:S(2)}) collective-permute-start(f32[7,32,4,128]{3,1,2,0:T(8,128)} %copy.65), channel_id=1, source_target_pairs={{0,1},{16,17},{32,33},{48,49},{64,65},{80,81},{96,97},{112,113},{1... | collective-permute-start | bytes 1376264 | tf_op jit(solution)/shard_map/ppermute | solution.py:115
  22.8 2.6 %fusion.66 = (f32[7,32,16,4]{3,2,1,0:T(8,128)}, f32[7,32,16,4]{3,2,1,0:T(8,128)}) fusion(f32[7,32,16,128]{3,2,1,0:T(8,128)S(1)} %constant_dynamic-update-slice_fusion), kind=kLoop, calls=%fused_computation.185 | loop fusion | bytes 229376 | tf_op jit(solution)/shard_map/slice | solution.py:124
  25.4 2.9 %copy.67 = f32[7,32,16,4]{1,2,3,0:T(8,128)} copy(f32[7,32,16,4]{3,2,1,0:T(8,128)} %get-tuple-element.52) | data formatting | bytes 114688
  28.3 2.9 %copy.68 = f32[7,32,16,4]{1,2,3,0:T(8,128)} copy(f32[7,32,16,4]{3,2,1,0:T(8,128)} %get-tuple-element.53) | data formatting | bytes 114688
  31.3 5.6 %collective-permute-start.4 = (f32[7,32,16,4]{1,2,3,0:T(8,128)}, f32[7,32,16,4]{1,2,3,0:T(8,128)S(1)}, u32[]{:S(2)}, u32[]{:S(2)}) collective-permute-start(f32[7,32,16,4]{1,2,3,0:T(8,128)} %copy.68), channel_id=1, source_target_pairs={{0,240},{16,0},{32,16},{48,32},{64,48},{80,64},{96,80},{112,96},{1... | collective-permute-start | bytes 172040 | tf_op jit(solution)/shard_map/ppermute | solution.py:115
  40.3 1.9 %collective-permute-start.5 = (f32[7,32,4,4]{3,1,2,0:T(8,128)}, f32[7,32,4,4]{3,1,2,0:T(8,128)}, u32[]{:S(2)}, u32[]{:S(2)}) collective-permute-start(f32[7,32,4,4]{3,1,2,0:T(8,128)} %copy.69), channel_id=1, source_target_pairs={{1,16},{17,32},{33,48},{49,64},{65,80},{81,96},{97,112},{113,128},... | collective-permute-start | bytes 43016 | tf_op jit(solution)/shard_map/ppermute | solution.py:115
  42.2 2.0 %copy.48 = f32[7,32,16,4]{3,2,1,0:T(8,128)} copy(f32[7,32,16,4]{1,2,3,0:T(8,128)S(1)} %collective-permute-done.3) | data formatting | bytes 114688 | tf_op jit(solution)/shard_map/ppermute | solution.py:115
  44.2 3.8 %collective-permute-start.6 = (f32[7,32,4,128]{3,1,2,0:T(8,128)}, f32[7,32,4,128]{3,1,2,0:T(8,128)}, u32[]{:S(2)}, u32[]{:S(2)}) collective-permute-start(f32[7,32,4,128]{3,1,2,0:T(8,128)} %copy.70), channel_id=1, source_target_pairs={{1,0},{17,16},{33,32},{49,48},{65,64},{81,80},{97,96},{113,112},{1... | collective-permute-start | bytes 1376264 | tf_op jit(solution)/shard_map/ppermute | solution.py:115
  48.0 2.0 %copy.49 = f32[7,32,16,4]{3,2,1,0:T(8,128)} copy(f32[7,32,16,4]{1,2,3,0:T(8,128)S(1)} %collective-permute-done.4) | data formatting | bytes 114688 | tf_op jit(solution)/shard_map/ppermute | solution.py:115
  50.0 2.7 %multiply_bitcast_fusion.11 = (f32[32,16,129]{2,1,0:T(8,128)}, f32[1,32,16,129]{3,2,1,0:T(8,128)S(1)}, f32[32,16,129]{2,1,0:T(8,128)}) fusion(f32[7,32,16,128]{3,2,1,0:T(8,128)S(1)} %constant_dynamic-update-slice_fusion, f32[7,32,16,4]{3,2,1,0:T(8,128)} %copy.48, f32[7,32,16,4]{3,2,1,0:T(8,128)} %copy.49), kind=kLoop, calls=%fused_computation.143 | loop fusion | flops 528384 | bytes 2742272 | tf_op jit(solution)/shard_map/mul | solution.py:33
  52.7 1.5 %pad_maximum_fusion.1 = f32[7,32,16,136]{3,2,1,0:T(8,128)S(1)} fusion(f32[7,32,16,4]{3,2,1,0:T(8,128)S(1)} %copy-done.1, f32[7,32,16,128]{3,2,1,0:T(8,128)S(1)} %constant_dynamic-update-slice_fusion, f32[7,32,16,4]{3,2,1,0:T(8,128)S(1)} %copy-done), kind=kLoop, calls=%fused_computation.1 | loop fusion | flops 974848 | bytes 3899392 | tf_op jit(solution)/shard_map/concatenate | solution.py:135
  57.8 2.1 %copy.57 = f32[7,32,16,136]{3,1,2,0:T(8,128)S(1)} copy(f32[7,32,16,136]{3,2,1,0:T(8,128)S(1)} %pad_maximum_fusion.1) | data formatting | bytes 3899392 | tf_op jit(solution)/shard_map/concatenate | solution.py:135
  63.1 6.0 %collective-permute-start.7 = (f32[7,32,4,4]{3,1,2,0:T(8,128)S(1)}, f32[7,32,4,4]{3,1,2,0:T(8,128)S(1)}, u32[]{:S(2)}, u32[]{:S(2)}) collective-permute-start(f32[7,32,4,4]{3,1,2,0:T(8,128)S(1)} %copy-done.33), channel_id=1, source_target_pairs={{1,240},{17,0},{33,16},{49,32},{65,48},{81,64},{97,80},{113,96},{1... | collective-permute-start | bytes 43016 | tf_op jit(solution)/shard_map/ppermute | solution.py:115
  69.2 1.6 %pad_maximum_fusion.2 = f32[7,32,4,136]{3,1,2,0:T(8,128)S(1)} fusion(f32[7,32,4,4]{3,1,2,0:T(8,128)} %collective-permute-done.2, f32[7,32,4,128]{3,1,2,0:T(8,128)} %collective-permute-done.1, f32[7,32,4,4]{3,1,2,0:T(8,128)S(1)} %collective-permute-done), kind=kLoop, calls=%fused_computation.63 | loop fusion | flops 243712 | bytes 974848 | tf_op jit(solution)/shard_map/concatenate | solution.py:134
  71.4 8.0 %collective-permute-done.7 = f32[7,32,4,4]{3,1,2,0:T(8,128)S(1)} collective-permute-done((f32[7,32,4,4]{3,1,2,0:T(8,128)S(1)}, f32[7,32,4,4]{3,1,2,0:T(8,128)S(1)}, u32[]{:S(2)}, u32[]{:S(2)}) %collective-permute-start.7) | collective-permute-done | bytes 14368 | tf_op jit(solution)/shard_map/ppermute | solution.py:115
  79.4 1.6 %pad_maximum_fusion.3 = f32[7,32,4,136]{3,1,2,0:T(8,128)S(1)} fusion(f32[7,32,4,4]{3,1,2,0:T(8,128)S(1)} %collective-permute-done.7, f32[7,32,4,128]{3,1,2,0:T(8,128)} %collective-permute-done.6, f32[7,32,4,4]{3,1,2,0:T(8,128)} %collective-permute-done.5), kind=kLoop, calls=%fused_computation.64 | loop fusion | flops 243712 | bytes 974848 | tf_op jit(solution)/shard_map/concatenate | solution.py:136
  81.6 3.2 %pad_maximum_fusion = f32[7,32,24,136]{3,2,1,0:T(8,128)S(1)} fusion(f32[7,32,4,136]{3,2,1,0:T(4,128)S(1)} %copy.54, f32[7,32,16,4]{3,2,1,0:T(8,128)S(1)} %copy-done.1, f32[7,32,16,128]{3,2,1,0:T(8,128)S(1)} %constant_dynamic-update-slice_fusion, f32[7,32,16,4]{3,2,1,0:T(8,128)S(1)} %copy-done, f32[7,32,4,136]{3,2,1,0:T(4,128)S(1)} %copy.53), kind=kLoop, calls=%fused_computation | loop fusion | flops 2924544 | bytes 5849088 | tf_op jit(solution)/shard_map/concatenate | solution.py:137
  89.9 1.6 %multiply_bitcast_fusion.1 = (f32[32,23,132]{2,1,0:T(8,128)S(1)}, f32[32,23,132]{2,1,0:T(8,128)S(1)}, f32[32,23,132]{2,1,0:T(8,128)S(1)}, f32[32,23,132]{2,1,0:T(8,128)S(1)}, f32[32,23,132]{2,1,0:T(8,128)}) fusion(f32[7,32,24,136]{3,2,1,0:T(8,128)S(1)} %pad_maximum_fusion), kind=kLoop, calls=%fused_computation.90 | loop fusion | flops 1457280 | bytes 3108864 | tf_op jit(solution)/shard_map/mul | solution.py:45
  92.4 1.7 %multiply_bitcast_fusion.13 = (f32[32,19,128]{2,1,0:T(8,128)}, f32[32,19,128]{2,1,0:T(8,128)}, f32[32,19,128]{2,1,0:T(8,128)}, f32[32,19,128]{2,1,0:T(8,128)}, f32[32,19,128]{2,1,0:T(8,128)}) fusion(f32[7,32,24,136]{3,2,1,0:T(8,128)S(1)} %pad_maximum_fusion), kind=kLoop, calls=%fused_computation.155 | loop fusion | flops 1167360 | bytes 2490368 | tf_op jit(solution)/shard_map/mul | solution.py:45
  101.5 1.8 %fusion.16 = f32[2,32,21,132]{3,2,1,0:T(8,128)S(1)} fusion(f32[7,32,24,136]{3,2,1,0:T(8,128)S(1)} %pad_maximum_fusion, f32[32,21,132]{2,1,0:T(8,128)S(1)} %get-tuple-element.35, f32[32,21,132]{2,1,0:T(8,128)S(1)} %get-tuple-element.37, f32[32,21,132]{2,1,0:T(8,128)S(1)} %get-tuple-element.36, f32[32,21,132]{2,1,0:T(8,128)S(1)} %get-tuple-element.38, ...), kind=kLoop, calls=%fused_computation.32 | loop fusion | flops 1419264 | bytes 5322240 | tf_op jit(solution)/shard_map/mul | solution.py:32
  114.0 2.2 %fusion.2 = f32[2,32,20,132]{3,2,1,0:T(8,128)S(1)} fusion(f32[2,32,23,132]{3,2,1,0:T(8,128)S(1)} %fusion.5, f32[2,32,20,135]{3,2,1,0:T(8,128)S(1)} %fusion.10, f32[2,31,20,132]{3,2,1,0:T(8,128)S(1)} %fusion.23, f32[7,32,24,136]{3,2,1,0:T(8,128)S(1)} %pad_maximum_fusion, f32[32,20,132]{2,1,0:T(8,128)S(1)} %bitcast.120, f32[32,20,132]{2,1,0:T(8,128)S(1)} %slice.650, ...), kind=kLoop, calls=%fused_computation.5 | loop fusion | flops 3041280 | bytes 10116480 | tf_op jit(solution)/shard_map/add | solution.py:98
  (151 shorter events, 49.0 us)
Async XLA Ops:
  0.6 3.0 %copy-start.34 = (f32[32,16,128]{2,1,0:T(8,128)S(1)}, f32[32,16,128]{2,1,0:T(8,128)}, u32[]{:S(2)}) copy-start(f32[32,16,128]{2,1,0:T(8,128)} %param.13) | copy-start | bytes 786436
  0.6 3.1 %copy-start.35 = (f32[32,16,128]{2,1,0:T(8,128)S(1)}, f32[32,16,128]{2,1,0:T(8,128)}, u32[]{:S(2)}) copy-start(f32[32,16,128]{2,1,0:T(8,128)} %param.9) | copy-start | bytes 786436
  0.7 3.1 %copy-start.36 = (f32[32,16,128]{2,1,0:T(8,128)S(1)}, f32[32,16,128]{2,1,0:T(8,128)}, u32[]{:S(2)}) copy-start(f32[32,16,128]{2,1,0:T(8,128)} %param.10) | copy-start | bytes 786436
  0.7 3.1 %copy-start.28 = (s32[32,16,128]{2,1,0:T(8,128)S(1)}, s32[32,16,128]{2,1,0:T(8,128)}, u32[]{:S(2)}) copy-start(s32[32,16,128]{2,1,0:T(8,128)} %param.11) | copy-start | bytes 786436
  6.3 56.8 %collective-permute-start = (f32[7,32,4,4]{3,1,2,0:T(8,128)}, f32[7,32,4,4]{3,1,2,0:T(8,128)S(1)}, u32[]{:S(2)}, u32[]{:S(2)}) collective-permute-start(f32[7,32,4,4]{3,1,2,0:T(8,128)} %copy.64), channel_id=1, source_target_pairs={{0,17},{16,33},{32,49},{48,65},{64,81},{80,97},{96,113},{112,129},... | collective-permute-start | bytes 43016 | tf_op jit(solution)/shard_map/ppermute | solution.py:115
  10.4 58.8 %collective-permute-start.2 = (f32[7,32,4,4]{3,1,2,0:T(8,128)}, f32[7,32,4,4]{3,1,2,0:T(8,128)}, u32[]{:S(2)}, u32[]{:S(2)}) collective-permute-start(f32[7,32,4,4]{3,1,2,0:T(8,128)} %copy.66), channel_id=1, source_target_pairs={{0,241},{16,1},{32,17},{48,33},{64,49},{80,65},{96,81},{112,97},{1... | collective-permute-start | bytes 43016 | tf_op jit(solution)/shard_map/ppermute | solution.py:115
  20.5 48.6 %collective-permute-start.1 = (f32[7,32,4,128]{3,1,2,0:T(8,128)}, f32[7,32,4,128]{3,1,2,0:T(8,128)}, u32[]{:S(2)}, u32[]{:S(2)}) collective-permute-start(f32[7,32,4,128]{3,1,2,0:T(8,128)} %copy.65), channel_id=1, source_target_pairs={{0,1},{16,17},{32,33},{48,49},{64,65},{80,81},{96,97},{112,113},{1... | collective-permute-start | bytes 1376264 | tf_op jit(solution)/shard_map/ppermute | solution.py:115
  28.3 11.9 %collective-permute-start.3 = (f32[7,32,16,4]{1,2,3,0:T(8,128)}, f32[7,32,16,4]{1,2,3,0:T(8,128)S(1)}, u32[]{:S(2)}, u32[]{:S(2)}) collective-permute-start(f32[7,32,16,4]{1,2,3,0:T(8,128)} %copy.67), channel_id=1, source_target_pairs={{0,16},{16,32},{32,48},{48,64},{64,80},{80,96},{96,112},{112,128},... | collective-permute-start | bytes 172040 | tf_op jit(solution)/shard_map/ppermute | solution.py:115
  31.3 6.4 %copy-start.15 = (f32[7,32,4,4]{3,2,1,0:T(4,128)S(1)}, f32[7,32,4,4]{3,2,1,0:T(4,128)}, u32[]{:S(2)}) copy-start(f32[7,32,4,4]{3,2,1,0:T(4,128)} %get-tuple-element.47) | copy-start | bytes 43012
  31.3 7.3 %copy-start.14 = (f32[7,32,4,4]{3,2,1,0:T(4,128)S(1)}, f32[7,32,4,4]{3,2,1,0:T(4,128)}, u32[]{:S(2)}) copy-start(f32[7,32,4,4]{3,2,1,0:T(4,128)} %get-tuple-element.49) | copy-start | bytes 43012
  31.3 8.1 %copy-start.16 = (f32[7,32,4,128]{3,2,1,0:T(4,128)S(1)}, f32[7,32,4,128]{3,2,1,0:T(4,128)}, u32[]{:S(2)}) copy-start(f32[7,32,4,128]{3,2,1,0:T(4,128)} %get-tuple-element.51) | copy-start | bytes 1376260
  31.3 12.9 %collective-permute-start.4 = (f32[7,32,16,4]{1,2,3,0:T(8,128)}, f32[7,32,16,4]{1,2,3,0:T(8,128)S(1)}, u32[]{:S(2)}, u32[]{:S(2)}) collective-permute-start(f32[7,32,16,4]{1,2,3,0:T(8,128)} %copy.68), channel_id=1, source_target_pairs={{0,240},{16,0},{32,16},{48,32},{64,48},{80,64},{96,80},{112,96},{1... | collective-permute-start | bytes 172040 | tf_op jit(solution)/shard_map/ppermute | solution.py:115
  40.3 31.1 %collective-permute-start.5 = (f32[7,32,4,4]{3,1,2,0:T(8,128)}, f32[7,32,4,4]{3,1,2,0:T(8,128)}, u32[]{:S(2)}, u32[]{:S(2)}) collective-permute-start(f32[7,32,4,4]{3,1,2,0:T(8,128)} %copy.69), channel_id=1, source_target_pairs={{1,16},{17,32},{33,48},{49,64},{65,80},{81,96},{97,112},{113,128},... | collective-permute-start | bytes 43016 | tf_op jit(solution)/shard_map/ppermute | solution.py:115
  44.2 35.2 %collective-permute-start.6 = (f32[7,32,4,128]{3,1,2,0:T(8,128)}, f32[7,32,4,128]{3,1,2,0:T(8,128)}, u32[]{:S(2)}, u32[]{:S(2)}) collective-permute-start(f32[7,32,4,128]{3,1,2,0:T(8,128)} %copy.70), channel_id=1, source_target_pairs={{1,0},{17,16},{33,32},{49,48},{65,64},{81,80},{97,96},{113,112},{1... | collective-permute-start | bytes 1376264 | tf_op jit(solution)/shard_map/ppermute | solution.py:115
  50.0 2.7 %copy-start = (f32[7,32,16,4]{3,2,1,0:T(8,128)S(1)}, f32[7,32,16,4]{3,2,1,0:T(8,128)}, u32[]{:S(2)}) copy-start(f32[7,32,16,4]{3,2,1,0:T(8,128)} %copy.48) | copy-start | bytes 172036
  50.0 2.7 %copy-start.1 = (f32[7,32,16,4]{3,2,1,0:T(8,128)S(1)}, f32[7,32,16,4]{3,2,1,0:T(8,128)}, u32[]{:S(2)}) copy-start(f32[7,32,16,4]{3,2,1,0:T(8,128)} %copy.49) | copy-start | bytes 172036
  59.9 3.2 %copy-start.33 = (f32[7,32,4,4]{3,1,2,0:T(8,128)S(1)}, f32[7,32,4,4]{3,1,2,0:T(8,128)}, u32[]{:S(2)}) copy-start(f32[7,32,4,4]{3,1,2,0:T(8,128)} %copy.71) | copy-start | bytes 43012
  63.1 8.3 %copy-start.12 = (f32[7,32,4,4]{3,1,2,0:T(8,128)}, f32[7,32,4,4]{3,1,2,0:T(8,128)S(1)}, u32[]{:S(2)}) copy-start(f32[7,32,4,4]{3,1,2,0:T(8,128)S(1)} %collective-permute-done) | copy-start | bytes 43012
  63.1 16.3 %collective-permute-start.7 = (f32[7,32,4,4]{3,1,2,0:T(8,128)S(1)}, f32[7,32,4,4]{3,1,2,0:T(8,128)S(1)}, u32[]{:S(2)}, u32[]{:S(2)}) collective-permute-start(f32[7,32,4,4]{3,1,2,0:T(8,128)S(1)} %copy-done.33), channel_id=1, source_target_pairs={{1,240},{17,0},{33,16},{49,32},{65,48},{81,64},{97,80},{113,96},{1... | collective-permute-start | bytes 43016 | tf_op jit(solution)/shard_map/ppermute | solution.py:115
  110.3 1.4 %copy-start.9 = (f32[32,16,129]{2,1,0:T(8,128)S(1)}, f32[32,16,129]{2,1,0:T(8,128)}, u32[]{:S(2)}) copy-start(f32[32,16,129]{2,1,0:T(8,128)} %get-tuple-element.58) | copy-start | bytes 792580
  111.7 1.3 %copy-start.20 = (f32[32,17,128]{2,1,0:T(8,128)S(1)}, f32[32,17,128]{2,1,0:T(8,128)}, u32[]{:S(2)}) copy-start(f32[32,17,128]{2,1,0:T(8,128)} %copy.60) | copy-start | bytes 835588
  114.0 2.2 %copy-start.27 = (f32[32,16,128]{2,1,0:T(8,128)S(1)}, f32[32,16,128]{2,1,0:T(8,128)}, u32[]{:S(2)}) copy-start(f32[32,16,128]{2,1,0:T(8,128)} %get-tuple-element.66) | copy-start | bytes 786436
  117.8 1.3 %copy-start.26 = (f32[32,19,128]{2,1,0:T(8,128)S(1)}, f32[32,19,128]{2,1,0:T(8,128)}, u32[]{:S(2)}) copy-start(f32[32,19,128]{2,1,0:T(8,128)} %get-tuple-element.14) | copy-start | bytes 933892
  118.8 1.4 %copy-start.6 = (f32[32,16,131]{2,1,0:T(8,128)S(1)}, f32[32,16,131]{2,1,0:T(8,128)}, u32[]{:S(2)}) copy-start(f32[32,16,131]{2,1,0:T(8,128)} %get-tuple-element.44) | copy-start | bytes 804868
  (21 other events, 23.2 us)

commit v2 on v1

v2 whole, which is shorter than its diff:
```python
import functools

import jax
import jax.numpy as jnp
from jax import lax
from jax.experimental import pallas as pl
from jax.experimental.pallas import tpu as pltpu
from jax.sharding import PartitionSpec as P

horizontal_mix = 0.05
vertical_mix = 0.2

PAD = 8
KC = 2
N_FIELDS = 7
N_TRACERS = 4
U, V, M = 4, 5, 6
MESH = pl.DeviceIdType.MESH


def coefficients(speed):
    magnitude = jnp.abs(speed)
    return (
        (-speed - magnitude) / 12.0,
        (7.0 * speed + 3.0 * magnitude) / 12.0 + horizontal_mix,
        (7.0 * speed - 3.0 * magnitude) / 12.0 - horizontal_mix,
        (-speed + magnitude) / 12.0,
    )


def shift_x(c, left, right, lane, cols):
    cm1 = pltpu.roll(jnp.where(lane >= cols - 1, left, c), 1, 2)
    cm2 = pltpu.roll(jnp.where(lane >= cols - 2, left, c), 2, 2)
    cp1 = pltpu.roll(jnp.where(lane < 1, right, c), cols - 1, 2)
    cp2 = pltpu.roll(jnp.where(lane < 2, right, c), cols - 2, 2)
    return cm2, cm1, cp1, cp2


def kernel(n_ew, n_ns, levels, rows, cols,
           t_hbm, s_hbm, ct_hbm, cs_hbm, u_hbm, v_hbm, wet_ref,
           o_t, o_s, o_ct, o_cs,
           b0, x0, ts0, rt0, b1, x1, ts1, rt1, w, oz, load_sem, send_sem, recv_sem):
    ew = lax.axis_index("ew")
    ns = lax.axis_index("ns")
    east = (lax.rem(ew + 1, n_ew), ns)
    west = (lax.rem(ew + n_ew - 1, n_ew), ns)
    north = (ew, jnp.minimum(ns + 1, n_ns - 1))
    south = (ew, jnp.maximum(ns - 1, 0))
    has_north = ns < n_ns - 1
    has_south = ns > 0
    inner = pl.ds(PAD, rows)
    lev = pl.ds(1, levels)

    loads = []
    for f, src in enumerate((t_hbm, s_hbm, ct_hbm, cs_hbm, u_hbm, v_hbm)):
        cp = pltpu.make_async_copy(src, b0.at[f, lev, inner, :], load_sem.at[f])
        cp.start()
        loads.append(cp)

    for buf, nf in ((b0, N_FIELDS), (b1, N_TRACERS)):
        zl = jnp.zeros((nf, 1, rows + 2 * PAD, cols), jnp.float32)
        buf[:, pl.ds(0, 1), :, :] = zl
        buf[:, pl.ds(levels + 1, 1), :, :] = zl
        zr = jnp.zeros((nf, levels, PAD, cols), jnp.float32)
        buf[:, lev, pl.ds(0, PAD), :] = zr
        buf[:, lev, pl.ds(PAD + rows, PAD), :] = zr
    b0[M, lev, inner, :] = wet_ref[...].astype(jnp.float32)
    oz[pl.ds(0, 1), :, :] = jnp.zeros((1, rows, cols), jnp.float32)
    for cp in loads:
        cp.wait()

    barrier = pltpu.get_barrier_semaphore()
    pl.semaphore_signal(barrier, 1, device_id=east, device_id_type=MESH)
    pl.semaphore_signal(barrier, 1, device_id=west, device_id_type=MESH)

    @pl.when(has_north)
    def _():
        pl.semaphore_signal(barrier, 1, device_id=north, device_id_type=MESH)

    @pl.when(has_south)
    def _():
        pl.semaphore_signal(barrier, 1, device_id=south, device_id_type=MESH)

    peers = 2 + has_north.astype(jnp.int32) + has_south.astype(jnp.int32)
    pl.semaphore_wait(barrier, peers)

    def edge_copy(r, d, dev):
        buf, ts, rt = (b0, ts0, rt0) if r == 0 else (b1, ts1, rt1)
        if d == 0:
            src = buf.at[:, lev, pl.ds(PAD + rows - 2, 2), :]
            dst = buf.at[:, lev, pl.ds(PAD - 2, 2), :]
        elif d == 1:
            src = buf.at[:, lev, pl.ds(PAD, 2), :]
            dst = buf.at[:, lev, pl.ds(PAD + rows, 2), :]
        elif d == 2:
            src = ts.at[:, pl.ds(cols - 2, 2), :]
            dst = rt.at[:, pl.ds(cols - 2, 2), :]
        else:
            src = ts.at[:, pl.ds(0, 2), :]
            dst = rt.at[:, pl.ds(0, 2), :]
        return pltpu.make_async_remote_copy(
            src_ref=src, dst_ref=dst, send_sem=send_sem.at[r, d], recv_sem=recv_sem.at[r, d],
            device_id=dev, device_id_type=MESH,
        )

    def pack_columns(r):
        buf, ts = (b0, ts0) if r == 0 else (b1, ts1)
        for f in range(ts.shape[0]):
            ts[f] = buf[f, lev, inner, :].reshape(levels * rows, cols).T

    def unpack_columns(r):
        x, rt = (x0, rt0) if r == 0 else (x1, rt1)
        for f in range(rt.shape[0]):
            x[f] = rt[f].T.reshape(levels, rows, cols)

    def exchange(r):
        pack_columns(r)
        outgoing = ((0, north, has_north), (1, south, has_south), (2, east, None), (3, west, None))
        incoming = ((0, south, has_south), (1, north, has_north), (2, west, None), (3, east, None))
        for d, dev, cond in outgoing:
            if cond is None:
                edge_copy(r, d, dev).start()
            else:
                pl.when(cond)(lambda d=d, dev=dev: edge_copy(r, d, dev).start())
        for d, dev, cond in incoming:
            if cond is None:
                edge_copy(r, d, dev).wait_recv()
            else:
                pl.when(cond)(lambda d=d, dev=dev: edge_copy(r, d, dev).wait_recv())
        unpack_columns(r)

    def finish_sends(r):
        outgoing = ((0, north, has_north), (1, south, has_south), (2, east, None), (3, west, None))
        for d, dev, cond in outgoing:
            if cond is None:
                edge_copy(r, d, dev).wait_send()
            else:
                pl.when(cond)(lambda d=d, dev=dev: edge_copy(r, d, dev).wait_send())

    exchange(0)

    lane = lax.broadcasted_iota(jnp.int32, (KC, rows, cols), 2)

    def rows_at(buf, f, k0, d):
        return buf[f, pl.ds(1 + k0, KC), pl.ds(PAD + d, rows), :]

    def weights_body(i, carry):
        k0 = pl.multiple_of(i * KC, KC)
        kk = pl.ds(k0, KC)
        u0 = rows_at(b0, U, k0, 0)
        um2, um1, up1, _ = shift_x(u0, x0[U, kk], x0[U, kk], lane, cols)
        m0 = rows_at(b0, M, k0, 0)
        mm2, mm1, mp1, mp2 = shift_x(m0, x0[M, kk], x0[M, kk], lane, cols)
        v0 = rows_at(b0, V, k0, 0)
        vm1, vm2, vp1 = rows_at(b0, V, k0, -1), rows_at(b0, V, k0, -2), rows_at(b0, V, k0, 1)
        nm2, nm1 = rows_at(b0, M, k0, -2), rows_at(b0, M, k0, -1)
        np1, np2 = rows_at(b0, M, k0, 1), rows_at(b0, M, k0, 2)
        for base, (s_m2, s_m1, s_0, s_p1), (q_m2, q_m1, q_0, q_p1, q_p2) in (
            (0, (um2, um1, u0, up1), (mm2, mm1, m0, mp1, mp2)),
            (10, (vm2, vm1, v0, vp1), (nm2, nm1, m0, np1, np2)),
        ):
            a0 = coefficients(s_0)
            am1 = coefficients(s_m1)
            o0 = q_0 * q_p1
            om1 = q_m1 * q_0
            for k in range(4):
                w[base + k, kk] = o0 * a0[k]
                w[base + 4 + k, kk] = om1 * am1[k]
            w[base + 8, kk] = (q_p1 * q_p2) * coefficients(s_p1)[0]
            w[base + 9, kk] = (q_m2 * q_m1) * coefficients(s_m2)[3]
        m_up = b0[M, pl.ds(2 + k0, KC), inner, :]
        oz[pl.ds(1 + k0, KC)] = vertical_mix * (m0 * m_up)
        return carry

    lax.fori_loop(0, levels // KC, weights_body, 0)

    def step(src, xh, f, k0, forward):
        kk = pl.ds(k0, KC)
        c = rows_at(src, f, k0, 0)
        cm2, cm1, cp1, cp2 = shift_x(c, xh[f, kk], xh[f, kk], lane, cols)
        ym2, ym1 = rows_at(src, f, k0, -2), rows_at(src, f, k0, -1)
        yp1, yp2 = rows_at(src, f, k0, 1), rows_at(src, f, k0, 2)
        zm = src[f, pl.ds(k0, KC), inner, :]
        zp = src[f, pl.ds(2 + k0, KC), inner, :]
        oz_lo = oz[pl.ds(k0, KC)]
        oz_hi = oz[pl.ds(1 + k0, KC)]
        if forward:
            fxr = w[0, kk] * cm1 + w[1, kk] * c + w[2, kk] * cp1 + w[3, kk] * cp2
            fxl = w[4, kk] * cm2 + w[5, kk] * cm1 + w[6, kk] * c + w[7, kk] * cp1
            fyr = w[10, kk] * ym1 + w[11, kk] * c + w[12, kk] * yp1 + w[13, kk] * yp2
            fyl = w[14, kk] * ym2 + w[15, kk] * ym1 + w[16, kk] * c + w[17, kk] * yp1
            gl = oz_lo * (zm - c)
            gr = oz_hi * (c - zp)
            return c + (((fxl - fxr) + (fyl - fyr)) + (gl - gr))
        bx = (w[8, kk] * (cp2 - cp1) + w[1, kk] * (cp1 - c)
              + w[6, kk] * (c - cm1) + w[9, kk] * (cm1 - cm2))
        by = (w[18, kk] * (yp2 - yp1) + w[11, kk] * (yp1 - c)
              + w[16, kk] * (c - ym1) + w[19, kk] * (ym1 - ym2))
        bz = oz_hi * (zp - c) - oz_lo * (c - zm)
        return c + bx + by + bz

    def step1_body(i, carry):
        k0 = pl.multiple_of(i * KC, KC)
        for f in range(N_TRACERS):
            b1[f, pl.ds(1 + k0, KC), inner, :] = step(b0, x0, f, k0, f < 2)
        return carry

    lax.fori_loop(0, levels // KC, step1_body, 0)
    finish_sends(0)
    exchange(1)

    outs = (o_t, o_s, o_ct, o_cs)

    def step2_body(i, carry):
        k0 = pl.multiple_of(i * KC, KC)
        for f in range(N_TRACERS):
            outs[f][pl.ds(k0, KC)] = step(b1, x1, f, k0, f < 2)
        return carry

    lax.fori_loop(0, levels // KC, step2_body, 0)
    finish_sends(1)


def local(n_ew, n_ns, temp, salt, u_east, v_north, wet, cot_temp, cot_salt):
    levels, rows, cols = temp.shape
    f32 = jnp.float32
    any_spec = pl.BlockSpec(memory_space=pl.ANY)
    vmem_spec = pl.BlockSpec(memory_space=pltpu.VMEM)
    out = jax.ShapeDtypeStruct((levels, rows, cols), f32)
    call = pl.pallas_call(
        functools.partial(kernel, n_ew, n_ns, levels, rows, cols),
        out_shape=(out,) * 4,
        in_specs=[any_spec] * 6 + [vmem_spec],
        out_specs=(vmem_spec,) * 4,
        scratch_shapes=[
            pltpu.VMEM((N_FIELDS, levels + 2, rows + 2 * PAD, cols), f32),
            pltpu.VMEM((N_FIELDS, levels, rows, cols), f32),
            pltpu.VMEM((N_FIELDS, cols, levels * rows), f32),
            pltpu.VMEM((N_FIELDS, cols, levels * rows), f32),
            pltpu.VMEM((N_TRACERS, levels + 2, rows + 2 * PAD, cols), f32),
            pltpu.VMEM((N_TRACERS, levels, rows, cols), f32),
            pltpu.VMEM((N_TRACERS, cols, levels * rows), f32),
            pltpu.VMEM((N_TRACERS, cols, levels * rows), f32),
            pltpu.VMEM((20, levels, rows, cols), f32),
            pltpu.VMEM((levels + 1, rows, cols), f32),
            pltpu.SemaphoreType.DMA((6,)),
            pltpu.SemaphoreType.DMA((2, 4)),
            pltpu.SemaphoreType.DMA((2, 4)),
        ],
        compiler_params=pltpu.CompilerParams(
            collective_id=0, has_side_effects=True, vmem_limit_bytes=56 * 1024 * 1024
        ),
    )
    o_t, o_s, o_ct, o_cs = call(temp, salt, cot_temp, cot_salt, u_east, v_north, wet)
    return o_t, o_s, o_ct, o_cs


def solution(mesh):
    spec = P(None, "ns", "ew")
    n_ew = mesh.shape["ew"]
    n_ns = mesh.shape["ns"]
    return jax.shard_map(
        functools.partial(local, n_ew, n_ns), mesh=mesh,
        in_specs=(spec,) * 7, out_specs=(spec,) * 4, check_vma=False,
    )
```

time: 125 us -> 37.5 us (0.30)
  the two profiles are of different devices: /device:TPU:8 before, /device:TPU:3 now
where the time goes in v2:
time: 37.5 us; the launch traced here: 37.3 us
  Pallas kernels  32.2 us (86%)
  local copies, waits for them, and re-layouts  4.5 us (12%)
  between operations  0.65 us (2%)
    pallas_call x1, Pallas kernels, local(): call(temp, salt, cot_temp, cot_salt, u_east, v_north, wet)  32.2 us
    unnamed x10, local copies, waits for them, and re-layouts  4.5 us

profile of v2, /device:TPU:3, one launch (start us, length us, event | category | flops | bytes accessed | tf_op | source)
XLA Modules:
  0.0 37.3 jit_solution(7671081530931751104)
XLA Ops:
  0.6 32.2 %shard_map.102 = (f32[32,16,128]{2,1,0:T(8,128)}, f32[32,16,128]{2,1,0:T(8,128)}, f32[32,16,128]{2,1,0:T(8,128)}, f32[32,16,128]{2,1,0:T(8,128)}) custom-call(f32[32,16,128]{2,1,0:T(8,128)} %t_hbm.1, f32[32,16,128]{2,1,0:T(8,128)} %s_hbm.1, f32[32,16,128]{2,1,0:T(8,128)} %ct_hbm.1, f32[32,16,128]{2,1,0:T(8,128)} %cs_hbm.1, f32[32,16,128]{2,1,0:T(8,128)} %u_hbm.1, ...), custom_call_target="tpu_custom_call" | custom-call | tf_op jit(solution)/shard_map/pallas_call | solution.py:254
  32.8 0.0 copy-start.2
  32.8 1.7 %copy.15 = f32[32,16,128]{2,1,0:T(8,128)} copy(f32[32,16,128]{2,1,0:T(8,128)} %get-tuple-element.8) | data formatting | bytes 524288
  34.5 0.0 copy-done.2
  34.5 0.0 copy-start.1
  34.5 0.7 %copy.16 = f32[32,16,128]{2,1,0:T(8,128)} copy(f32[32,16,128]{2,1,0:T(8,128)S(1)} %copy-done.2) | data formatting | bytes 524288
  35.2 0.3 copy-done.1
  35.6 0.0 copy-start
  35.6 0.7 %copy.17 = f32[32,16,128]{2,1,0:T(8,128)} copy(f32[32,16,128]{2,1,0:T(8,128)S(1)} %copy-done.1) | data formatting | bytes 524288
  36.3 0.3 copy-done
  36.6 0.7 %copy.18 = f32[32,16,128]{2,1,0:T(8,128)} copy(f32[32,16,128]{2,1,0:T(8,128)S(1)} %copy-done) | data formatting | bytes 524288
Async XLA Ops:
  32.8 1.7 %copy-start.2 = (f32[32,16,128]{2,1,0:T(8,128)S(1)}, f32[32,16,128]{2,1,0:T(8,128)}, u32[]{:S(2)}) copy-start(f32[32,16,128]{2,1,0:T(8,128)} %get-tuple-element.9) | copy-start | bytes 786436
  34.5 1.0 %copy-start.1 = (f32[32,16,128]{2,1,0:T(8,128)S(1)}, f32[32,16,128]{2,1,0:T(8,128)}, u32[]{:S(2)}) copy-start(f32[32,16,128]{2,1,0:T(8,128)} %get-tuple-element.10) | copy-start | bytes 786436
  35.6 1.0 %copy-start = (f32[32,16,128]{2,1,0:T(8,128)S(1)}, f32[32,16,128]{2,1,0:T(8,128)}, u32[]{:S(2)}) copy-start(f32[32,16,128]{2,1,0:T(8,128)} %get-tuple-element.11) | copy-start | bytes 786436

commit v3 on v2

--- a/solution.py
+++ b/solution.py
@@ -13,8 +13,9 @@
 PAD = 8
 KC = 2
 N_FIELDS = 7
+X_FIELDS = 6
 N_TRACERS = 4
-U, V, M = 4, 5, 6
+U, M, V = 4, 5, 6
 MESH = pl.DeviceIdType.MESH
 
 
@@ -52,8 +53,9 @@
     lev = pl.ds(1, levels)
 
     loads = []
-    for f, src in enumerate((t_hbm, s_hbm, ct_hbm, cs_hbm, u_hbm, v_hbm)):
-        cp = pltpu.make_async_copy(src, b0.at[f, lev, inner, :], load_sem.at[f])
+    fields = ((0, t_hbm), (1, s_hbm), (2, ct_hbm), (3, cs_hbm), (U, u_hbm), (V, v_hbm))
+    for j, (f, src) in enumerate(fields):
+        cp = pltpu.make_async_copy(src, b0.at[f, lev, inner, :], load_sem.at[j])
         cp.start()
         loads.append(cp)
 
@@ -84,60 +86,61 @@
     peers = 2 + has_north.astype(jnp.int32) + has_south.astype(jnp.int32)
     pl.semaphore_wait(barrier, peers)
 
+    def group(r):
+        if r == 0:
+            return b0, ts0, rt0, x0, pl.ds(0, N_FIELDS), pl.ds(0, X_FIELDS)
+        g = pl.ds(2 * (r - 1), 2)
+        return b1, ts1, rt1, x1, g, g
+
     def edge_copy(r, d, dev):
-        buf, ts, rt = (b0, ts0, rt0) if r == 0 else (b1, ts1, rt1)
+        buf, ts, rt, _, fy, fx = group(r)
         if d == 0:
-            src = buf.at[:, lev, pl.ds(PAD + rows - 2, 2), :]
-            dst = buf.at[:, lev, pl.ds(PAD - 2, 2), :]
+            src = buf.at[fy, lev, pl.ds(PAD + rows - 2, 2), :]
+            dst = buf.at[fy, lev, pl.ds(PAD - 2, 2), :]
         elif d == 1:
-            src = buf.at[:, lev, pl.ds(PAD, 2), :]
-            dst = buf.at[:, lev, pl.ds(PAD + rows, 2), :]
+            src = buf.at[fy, lev, pl.ds(PAD, 2), :]
+            dst = buf.at[fy, lev, pl.ds(PAD + rows, 2), :]
         elif d == 2:
-            src = ts.at[:, pl.ds(cols - 2, 2), :]
-            dst = rt.at[:, pl.ds(cols - 2, 2), :]
+            src = ts.at[fx, pl.ds(cols - 2, 2), :]
+            dst = rt.at[fx, pl.ds(cols - 2, 2), :]
         else:
-            src = ts.at[:, pl.ds(0, 2), :]
-            dst = rt.at[:, pl.ds(0, 2), :]
+            src = ts.at[fx, pl.ds(0, 2), :]
+            dst = rt.at[fx, pl.ds(0, 2), :]
         return pltpu.make_async_remote_copy(
             src_ref=src, dst_ref=dst, send_sem=send_sem.at[r, d], recv_sem=recv_sem.at[r, d],
             device_id=dev, device_id_type=MESH,
         )
 
-    def pack_columns(r):
-        buf, ts = (b0, ts0) if r == 0 else (b1, ts1)
-        for f in range(ts.shape[0]):
+    def x_fields(r):
+        return range(X_FIELDS) if r == 0 else range(2 * (r - 1), 2 * r)
+
+    outgoing = ((0, north, has_north), (1, south, has_south), (2, east, None), (3, west, None))
+    incoming = ((0, south, has_south), (1, north, has_north), (2, west, None), (3, east, None))
+
+    def each(r, pairs, action):
+        for d, dev, cond in pairs:
+            if cond is None:
+                action(edge_copy(r, d, dev))
+            else:
+                pl.when(cond)(lambda d=d, dev=dev: action(edge_copy(r, d, dev)))
+
+    def send(r):
+        buf, ts = group(r)[:2]
+        for f in x_fields(r):
             ts[f] = buf[f, lev, inner, :].reshape(levels * rows, cols).T
-
-    def unpack_columns(r):
-        x, rt = (x0, rt0) if r == 0 else (x1, rt1)
-        for f in range(rt.shape[0]):
+        each(r, outgoing, lambda c: c.start())
+
+    def receive(r):
+        rt, x = group(r)[2:4]
+        each(r, incoming, lambda c: c.wait_recv())
+        for f in x_fields(r):
             x[f] = rt[f].T.reshape(levels, rows, cols)
 
-    def exchange(r):
-        pack_columns(r)
-        outgoing = ((0, north, has_north), (1, south, has_south), (2, east, None), (3, west, None))
-        incoming = ((0, south, has_south), (1, north, has_north), (2, west, None), (3, east, None))
-        for d, dev, cond in outgoing:
-            if cond is None:
-                edge_copy(r, d, dev).start()
-            else:
-                pl.when(cond)(lambda d=d, dev=dev: edge_copy(r, d, dev).start())
-        for d, dev, cond in incoming:
-            if cond is None:
-                edge_copy(r, d, dev).wait_recv()
-            else:
-                pl.when(cond)(lambda d=d, dev=dev: edge_copy(r, d, dev).wait_recv())
-        unpack_columns(r)
-
     def finish_sends(r):
-        outgoing = ((0, north, has_north), (1, south, has_south), (2, east, None), (3, west, None))
-        for d, dev, cond in outgoing:
-            if cond is None:
-                edge_copy(r, d, dev).wait_send()
-            else:
-                pl.when(cond)(lambda d=d, dev=dev: edge_copy(r, d, dev).wait_send())
-
-    exchange(0)
+        each(r, outgoing, lambda c: c.wait_send())
+
+    send(0)
+    receive(0)
 
     lane = lax.broadcasted_iota(jnp.int32, (KC, rows, cols), 2)
 
@@ -199,26 +202,37 @@
         bz = oz_hi * (zp - c) - oz_lo * (c - zm)
         return c + bx + by + bz
 
-    def step1_body(i, carry):
-        k0 = pl.multiple_of(i * KC, KC)
-        for f in range(N_TRACERS):
-            b1[f, pl.ds(1 + k0, KC), inner, :] = step(b0, x0, f, k0, f < 2)
-        return carry
-
-    lax.fori_loop(0, levels // KC, step1_body, 0)
+    outs = (o_t, o_s, o_ct, o_cs)
+
+    def step1_loop(g):
+        def body(i, carry):
+            k0 = pl.multiple_of(i * KC, KC)
+            for f in (2 * g, 2 * g + 1):
+                b1[f, pl.ds(1 + k0, KC), inner, :] = step(b0, x0, f, k0, g == 0)
+            return carry
+
+        lax.fori_loop(0, levels // KC, body, 0)
+
+    def step2_loop(g):
+        def body(i, carry):
+            k0 = pl.multiple_of(i * KC, KC)
+            for f in (2 * g, 2 * g + 1):
+                outs[f][pl.ds(k0, KC)] = step(b1, x1, f, k0, g == 0)
+            return carry
+
+        lax.fori_loop(0, levels // KC, body, 0)
+
+    step1_loop(0)
+    send(1)
+    step1_loop(1)
+    send(2)
     finish_sends(0)
-    exchange(1)
-
-    outs = (o_t, o_s, o_ct, o_cs)
-
-    def step2_body(i, carry):
-        k0 = pl.multiple_of(i * KC, KC)
-        for f in range(N_TRACERS):
-            outs[f][pl.ds(k0, KC)] = step(b1, x1, f, k0, f < 2)
-        return carry
-
-    lax.fori_loop(0, levels // KC, step2_body, 0)
+    receive(1)
+    step2_loop(0)
+    receive(2)
+    step2_loop(1)
     finish_sends(1)
+    finish_sends(2)
 
 
 def local(n_ew, n_ns, temp, salt, u_east, v_north, wet, cot_temp, cot_salt):
@@ -234,9 +248,9 @@
         out_specs=(vmem_spec,) * 4,
         scratch_shapes=[
             pltpu.VMEM((N_FIELDS, levels + 2, rows + 2 * PAD, cols), f32),
-            pltpu.VMEM((N_FIELDS, levels, rows, cols), f32),
-            pltpu.VMEM((N_FIELDS, cols, levels * rows), f32),
-            pltpu.VMEM((N_FIELDS, cols, levels * rows), f32),
+            pltpu.VMEM((X_FIELDS, levels, rows, cols), f32),
+            pltpu.VMEM((X_FIELDS, cols, levels * rows), f32),
+            pltpu.VMEM((X_FIELDS, cols, levels * rows), f32),
             pltpu.VMEM((N_TRACERS, levels + 2, rows + 2 * PAD, cols), f32),
             pltpu.VMEM((N_TRACERS, levels, rows, cols), f32),
             pltpu.VMEM((N_TRACERS, cols, levels * rows), f32),
@@ -244,8 +258,8 @@
             pltpu.VMEM((20, levels, rows, cols), f32),
             pltpu.VMEM((levels + 1, rows, cols), f32),
             pltpu.SemaphoreType.DMA((6,)),
-            pltpu.SemaphoreType.DMA((2, 4)),
-            pltpu.SemaphoreType.DMA((2, 4)),
+            pltpu.SemaphoreType.DMA((3, 4)),
+            pltpu.SemaphoreType.DMA((3, 4)),
         ],
         compiler_params=pltpu.CompilerParams(
             collective_id=0, has_side_effects=True, vmem_limit_bytes=56 * 1024 * 1024

time: 37.5 us -> 37 us (0.987)
  the two profiles are of different devices: /device:TPU:3 before, /device:TPU:8 now
where the time goes in v3:
time: 37 us; the launch traced here: 36.6 us
  Pallas kernels  31.4 us (85%)
  local copies, waits for them, and re-layouts  4.5 us (12%)
  between operations  0.65 us (2%)
    pallas_call x1, Pallas kernels, local(): call(temp, salt, cot_temp, cot_salt, u_east, v_north, wet)  31.4 us
    unnamed x10, local copies, waits for them, and re-layouts  4.5 us

profile of v3, /device:TPU:8, one launch (start us, length us, event | category | flops | bytes accessed | tf_op | source)
XLA Modules:
  0.0 36.6 jit_solution(14010842816976597073)
XLA Ops:
  0.6 31.4 %shard_map.102 = (f32[32,16,128]{2,1,0:T(8,128)}, f32[32,16,128]{2,1,0:T(8,128)}, f32[32,16,128]{2,1,0:T(8,128)}, f32[32,16,128]{2,1,0:T(8,128)}) custom-call(f32[32,16,128]{2,1,0:T(8,128)} %t_hbm.1, f32[32,16,128]{2,1,0:T(8,128)} %s_hbm.1, f32[32,16,128]{2,1,0:T(8,128)} %ct_hbm.1, f32[32,16,128]{2,1,0:T(8,128)} %cs_hbm.1, f32[32,16,128]{2,1,0:T(8,128)} %u_hbm.1, ...), custom_call_target="tpu_custom_call" | custom-call | tf_op jit(solution)/shard_map/pallas_call | solution.py:268
  32.0 0.0 copy-start.2
  32.0 1.7 %copy.15 = f32[32,16,128]{2,1,0:T(8,128)} copy(f32[32,16,128]{2,1,0:T(8,128)} %get-tuple-element.8) | data formatting | bytes 524288
  33.8 0.0 copy-done.2
  33.8 0.0 copy-start.1
  33.8 0.7 %copy.16 = f32[32,16,128]{2,1,0:T(8,128)} copy(f32[32,16,128]{2,1,0:T(8,128)S(1)} %copy-done.2) | data formatting | bytes 524288
  34.5 0.3 copy-done.1
  34.8 0.0 copy-start
  34.8 0.7 %copy.17 = f32[32,16,128]{2,1,0:T(8,128)} copy(f32[32,16,128]{2,1,0:T(8,128)S(1)} %copy-done.1) | data formatting | bytes 524288
  35.5 0.3 copy-done
  35.9 0.7 %copy.18 = f32[32,16,128]{2,1,0:T(8,128)} copy(f32[32,16,128]{2,1,0:T(8,128)S(1)} %copy-done) | data formatting | bytes 524288
Async XLA Ops:
  32.0 1.7 %copy-start.2 = (f32[32,16,128]{2,1,0:T(8,128)S(1)}, f32[32,16,128]{2,1,0:T(8,128)}, u32[]{:S(2)}) copy-start(f32[32,16,128]{2,1,0:T(8,128)} %get-tuple-element.9) | copy-start | bytes 786436
  33.8 1.0 %copy-start.1 = (f32[32,16,128]{2,1,0:T(8,128)S(1)}, f32[32,16,128]{2,1,0:T(8,128)}, u32[]{:S(2)}) copy-start(f32[32,16,128]{2,1,0:T(8,128)} %get-tuple-element.10) | copy-start | bytes 786436
  34.8 1.0 %copy-start = (f32[32,16,128]{2,1,0:T(8,128)S(1)}, f32[32,16,128]{2,1,0:T(8,128)}, u32[]{:S(2)}) copy-start(f32[32,16,128]{2,1,0:T(8,128)} %get-tuple-element.11) | copy-start | bytes 786436

commit v4 on v3

--- a/solution.py
+++ b/solution.py
@@ -14,8 +14,9 @@
 KC = 2
 N_FIELDS = 7
 X_FIELDS = 6
+Y_FIRST = 1
 N_TRACERS = 4
-U, M, V = 4, 5, 6
+U, M, V = 0, 5, 6
 MESH = pl.DeviceIdType.MESH
 
 
@@ -52,8 +53,20 @@
     inner = pl.ds(PAD, rows)
     lev = pl.ds(1, levels)
 
+    barrier = pltpu.get_barrier_semaphore()
+    pl.semaphore_signal(barrier, 1, device_id=east, device_id_type=MESH)
+    pl.semaphore_signal(barrier, 1, device_id=west, device_id_type=MESH)
+
+    @pl.when(has_north)
+    def _():
+        pl.semaphore_signal(barrier, 1, device_id=north, device_id_type=MESH)
+
+    @pl.when(has_south)
+    def _():
+        pl.semaphore_signal(barrier, 1, device_id=south, device_id_type=MESH)
+
     loads = []
-    fields = ((0, t_hbm), (1, s_hbm), (2, ct_hbm), (3, cs_hbm), (U, u_hbm), (V, v_hbm))
+    fields = ((1, t_hbm), (2, s_hbm), (3, ct_hbm), (4, cs_hbm), (U, u_hbm), (V, v_hbm))
     for j, (f, src) in enumerate(fields):
         cp = pltpu.make_async_copy(src, b0.at[f, lev, inner, :], load_sem.at[j])
         cp.start()
@@ -63,32 +76,27 @@
         zl = jnp.zeros((nf, 1, rows + 2 * PAD, cols), jnp.float32)
         buf[:, pl.ds(0, 1), :, :] = zl
         buf[:, pl.ds(levels + 1, 1), :, :] = zl
-        zr = jnp.zeros((nf, levels, PAD, cols), jnp.float32)
-        buf[:, lev, pl.ds(0, PAD), :] = zr
-        buf[:, lev, pl.ds(PAD + rows, PAD), :] = zr
+        zr = jnp.zeros((nf, levels, 2, cols), jnp.float32)
+
+        @pl.when(jnp.logical_not(has_south))
+        def _():
+            buf[:, lev, pl.ds(PAD - 2, 2), :] = zr
+
+        @pl.when(jnp.logical_not(has_north))
+        def _():
+            buf[:, lev, pl.ds(PAD + rows, 2), :] = zr
+
     b0[M, lev, inner, :] = wet_ref[...].astype(jnp.float32)
     oz[pl.ds(0, 1), :, :] = jnp.zeros((1, rows, cols), jnp.float32)
     for cp in loads:
         cp.wait()
 
-    barrier = pltpu.get_barrier_semaphore()
-    pl.semaphore_signal(barrier, 1, device_id=east, device_id_type=MESH)
-    pl.semaphore_signal(barrier, 1, device_id=west, device_id_type=MESH)
-
-    @pl.when(has_north)
-    def _():
-        pl.semaphore_signal(barrier, 1, device_id=north, device_id_type=MESH)
-
-    @pl.when(has_south)
-    def _():
-        pl.semaphore_signal(barrier, 1, device_id=south, device_id_type=MESH)
-
     peers = 2 + has_north.astype(jnp.int32) + has_south.astype(jnp.int32)
     pl.semaphore_wait(barrier, peers)
 
     def group(r):
         if r == 0:
-            return b0, ts0, rt0, x0, pl.ds(0, N_FIELDS), pl.ds(0, X_FIELDS)
+            return b0, ts0, rt0, x0, pl.ds(Y_FIRST, N_FIELDS - Y_FIRST), pl.ds(0, X_FIELDS)
         g = pl.ds(2 * (r - 1), 2)
         return b1, ts1, rt1, x1, g, g
 
@@ -208,7 +216,7 @@
         def body(i, carry):
             k0 = pl.multiple_of(i * KC, KC)
             for f in (2 * g, 2 * g + 1):
-                b1[f, pl.ds(1 + k0, KC), inner, :] = step(b0, x0, f, k0, g == 0)
+                b1[f, pl.ds(1 + k0, KC), inner, :] = step(b0, x0, f + 1, k0, g == 0)
             return carry
 
         lax.fori_loop(0, levels // KC, body, 0)

time: 37 us -> 35 us (0.946)
  Pallas kernels: 31.4 us -> 29.6 us
    pallas_call x1, Pallas kernels: 31.4 us -> 29.6 us  [local(): call(temp, salt, cot_temp, cot_salt, u_east, v_north, wet)]
where the time goes in v4:
time: 35 us; the launch traced here: 34.8 us
  Pallas kernels  29.6 us (85%)
  local copies, waits for them, and re-layouts  4.5 us (13%)
  between operations  0.65 us (2%)
    pallas_call x1, Pallas kernels, local(): call(temp, salt, cot_temp, cot_salt, u_east, v_north, wet)  29.6 us
    unnamed x10, local copies, waits for them, and re-layouts  4.5 us

profile of v4, /device:TPU:8, one launch (start us, length us, event | category | flops | bytes accessed | tf_op | source)
XLA Modules:
  0.0 34.8 jit_solution(6745592704744843516)
XLA Ops:
  0.6 29.6 %shard_map.102 = (f32[32,16,128]{2,1,0:T(8,128)}, f32[32,16,128]{2,1,0:T(8,128)}, f32[32,16,128]{2,1,0:T(8,128)}, f32[32,16,128]{2,1,0:T(8,128)}) custom-call(f32[32,16,128]{2,1,0:T(8,128)} %t_hbm.1, f32[32,16,128]{2,1,0:T(8,128)} %s_hbm.1, f32[32,16,128]{2,1,0:T(8,128)} %ct_hbm.1, f32[32,16,128]{2,1,0:T(8,128)} %cs_hbm.1, f32[32,16,128]{2,1,0:T(8,128)} %u_hbm.1, ...), custom_call_target="tpu_custom_call" | custom-call | tf_op jit(solution)/shard_map/pallas_call | solution.py:276
  30.3 0.0 copy-start.2
  30.3 1.7 %copy.15 = f32[32,16,128]{2,1,0:T(8,128)} copy(f32[32,16,128]{2,1,0:T(8,128)} %get-tuple-element.8) | data formatting | bytes 524288
  32.0 0.0 copy-done.2
  32.0 0.0 copy-start.1
  32.0 0.7 %copy.16 = f32[32,16,128]{2,1,0:T(8,128)} copy(f32[32,16,128]{2,1,0:T(8,128)S(1)} %copy-done.2) | data formatting | bytes 524288
  32.7 0.3 copy-done.1
  33.0 0.0 copy-start
  33.0 0.7 %copy.17 = f32[32,16,128]{2,1,0:T(8,128)} copy(f32[32,16,128]{2,1,0:T(8,128)S(1)} %copy-done.1) | data formatting | bytes 524288
  33.7 0.3 copy-done
  34.1 0.7 %copy.18 = f32[32,16,128]{2,1,0:T(8,128)} copy(f32[32,16,128]{2,1,0:T(8,128)S(1)} %copy-done) | data formatting | bytes 524288
Async XLA Ops:
  30.3 1.7 %copy-start.2 = (f32[32,16,128]{2,1,0:T(8,128)S(1)}, f32[32,16,128]{2,1,0:T(8,128)}, u32[]{:S(2)}) copy-start(f32[32,16,128]{2,1,0:T(8,128)} %get-tuple-element.9) | copy-start | bytes 786436
  32.0 1.0 %copy-start.1 = (f32[32,16,128]{2,1,0:T(8,128)S(1)}, f32[32,16,128]{2,1,0:T(8,128)}, u32[]{:S(2)}) copy-start(f32[32,16,128]{2,1,0:T(8,128)} %get-tuple-element.10) | copy-start | bytes 786436
  33.0 1.0 %copy-start = (f32[32,16,128]{2,1,0:T(8,128)S(1)}, f32[32,16,128]{2,1,0:T(8,128)}, u32[]{:S(2)}) copy-start(f32[32,16,128]{2,1,0:T(8,128)} %get-tuple-element.11) | copy-start | bytes 786436

commit v5 on v4

--- a/solution.py
+++ b/solution.py
@@ -40,7 +40,7 @@
 
 def kernel(n_ew, n_ns, levels, rows, cols,
            t_hbm, s_hbm, ct_hbm, cs_hbm, u_hbm, v_hbm, wet_ref,
-           o_t, o_s, o_ct, o_cs,
+           o_all,
            b0, x0, ts0, rt0, b1, x1, ts1, rt1, w, oz, load_sem, send_sem, recv_sem):
     ew = lax.axis_index("ew")
     ns = lax.axis_index("ns")
@@ -210,7 +210,6 @@
         bz = oz_hi * (zp - c) - oz_lo * (c - zm)
         return c + bx + by + bz
 
-    outs = (o_t, o_s, o_ct, o_cs)
 
     def step1_loop(g):
         def body(i, carry):
@@ -225,7 +224,7 @@
         def body(i, carry):
             k0 = pl.multiple_of(i * KC, KC)
             for f in (2 * g, 2 * g + 1):
-                outs[f][pl.ds(k0, KC)] = step(b1, x1, f, k0, g == 0)
+                o_all[f, pl.ds(k0, KC)] = step(b1, x1, f, k0, g == 0)
             return carry
 
         lax.fori_loop(0, levels // KC, body, 0)
@@ -243,6 +242,16 @@
     finish_sends(2)
 
 
+def split_kernel(stacked, o_t, o_s, o_ct, o_cs, sem):
+    copies = []
+    for f, dst in enumerate((o_t, o_s, o_ct, o_cs)):
+        cp = pltpu.make_async_copy(stacked.at[f], dst, sem.at[f])
+        cp.start()
+        copies.append(cp)
+    for cp in copies:
+        cp.wait()
+
+
 def local(n_ew, n_ns, temp, salt, u_east, v_north, wet, cot_temp, cot_salt):
     levels, rows, cols = temp.shape
     f32 = jnp.float32
@@ -251,9 +260,9 @@
     out = jax.ShapeDtypeStruct((levels, rows, cols), f32)
     call = pl.pallas_call(
         functools.partial(kernel, n_ew, n_ns, levels, rows, cols),
-        out_shape=(out,) * 4,
+        out_shape=jax.ShapeDtypeStruct((N_TRACERS, levels, rows, cols), f32),
         in_specs=[any_spec] * 6 + [vmem_spec],
-        out_specs=(vmem_spec,) * 4,
+        out_specs=vmem_spec,
         scratch_shapes=[
             pltpu.VMEM((N_FIELDS, levels + 2, rows + 2 * PAD, cols), f32),
             pltpu.VMEM((X_FIELDS, levels, rows, cols), f32),
@@ -273,8 +282,14 @@
             collective_id=0, has_side_effects=True, vmem_limit_bytes=56 * 1024 * 1024
         ),
     )
-    o_t, o_s, o_ct, o_cs = call(temp, salt, cot_temp, cot_salt, u_east, v_north, wet)
-    return o_t, o_s, o_ct, o_cs
+    stacked = call(temp, salt, cot_temp, cot_salt, u_east, v_north, wet)
+    return pl.pallas_call(
+        split_kernel,
+        out_shape=(out,) * 4,
+        in_specs=[vmem_spec],
+        out_specs=(any_spec,) * 4,
+        scratch_shapes=[pltpu.SemaphoreType.DMA((4,))],
+    )(stacked)
 
 
 def solution(mesh):

time: 35 us -> 32.7 us (0.934)
  local copies, waits for them, and re-layouts: 4.5 us -> 0 us
  Pallas kernels: 29.6 us -> 31.9 us
    unnamed x10 -> x0, local copies, waits for them, and re-layouts: 4.5 us -> none
    pallas_call x1 -> x2, Pallas kernels: 29.6 us -> 31.9 us  [the longest x1 29.6 us: local(): stacked = call(temp, salt, cot_temp, cot_salt, u_east, v_north, wet)]
where the time goes in v5:
time: 32.7 us; the launch traced here: 32.5 us
  Pallas kernels  31.9 us (98%)
  between operations  0.64 us (2%)
    pallas_call x1, Pallas kernels, local(): stacked = call(temp, salt, cot_temp, cot_salt, u_east, v_north, wet)  29.6 us
    pallas_call x1, Pallas kernels, local(): pl.pallas_call(split_kernel, out_shape=(out,) * 4, in_specs=[vmem_spec],...  2.22 us

profile of v5, /device:TPU:8, one launch (start us, length us, event | category | flops | bytes accessed | tf_op | source)
XLA Modules:
  0.0 32.5 jit_solution(11198867667811739803)
XLA Ops:
  0.6 29.6 %shard_map.102.stacked = f32[4,32,16,128]{3,2,1,0:T(8,128)} custom-call(f32[32,16,128]{2,1,0:T(8,128)} %t_hbm.1, f32[32,16,128]{2,1,0:T(8,128)} %s_hbm.1, f32[32,16,128]{2,1,0:T(8,128)} %ct_hbm.1, f32[32,16,128]{2,1,0:T(8,128)} %cs_hbm.1, f32[32,16,128]{2,1,0:T(8,128)} %u_hbm.1, f32[32,16,128]{2,1,0:T(8,128)} %v_hbm.1, s32[32,16,128]{2,1,0:T(8,128)} %wet_ref.1), custom_call_target="tpu_custom_call" | custom-call | tf_op jit(solution)/shard_map/pallas_call | solution.py:285
  30.3 2.2 %shard_map.103 = (f32[32,16,128]{2,1,0:T(8,128)}, f32[32,16,128]{2,1,0:T(8,128)}, f32[32,16,128]{2,1,0:T(8,128)}, f32[32,16,128]{2,1,0:T(8,128)}) custom-call(f32[4,32,16,128]{3,2,1,0:T(8,128)} %shard_map.102.stacked), custom_call_target="tpu_custom_call" | custom-call | tf_op jit(solution)/shard_map/pallas_call | solution.py:286

commit v6 on v5

--- a/solution.py
+++ b/solution.py
@@ -14,9 +14,8 @@
 KC = 2
 N_FIELDS = 7
 X_FIELDS = 6
-Y_FIRST = 1
 N_TRACERS = 4
-U, M, V = 0, 5, 6
+U, M, V = 4, 5, 6
 MESH = pl.DeviceIdType.MESH
 
 
@@ -66,7 +65,7 @@
         pl.semaphore_signal(barrier, 1, device_id=south, device_id_type=MESH)
 
     loads = []
-    fields = ((1, t_hbm), (2, s_hbm), (3, ct_hbm), (4, cs_hbm), (U, u_hbm), (V, v_hbm))
+    fields = ((0, t_hbm), (1, s_hbm), (2, ct_hbm), (3, cs_hbm), (U, u_hbm), (V, v_hbm))
     for j, (f, src) in enumerate(fields):
         cp = pltpu.make_async_copy(src, b0.at[f, lev, inner, :], load_sem.at[j])
         cp.start()
@@ -96,8 +95,10 @@
 
     def group(r):
         if r == 0:
-            return b0, ts0, rt0, x0, pl.ds(Y_FIRST, N_FIELDS - Y_FIRST), pl.ds(0, X_FIELDS)
-        g = pl.ds(2 * (r - 1), 2)
+            return b0, ts0, rt0, x0, pl.ds(M, 2), pl.ds(U, 2)
+        if r == 1:
+            return b0, ts0, rt0, x0, pl.ds(0, N_TRACERS), pl.ds(0, N_TRACERS)
+        g = pl.ds(2 * (r - 2), 2)
         return b1, ts1, rt1, x1, g, g
 
     def edge_copy(r, d, dev):
@@ -120,7 +121,11 @@
         )
 
     def x_fields(r):
-        return range(X_FIELDS) if r == 0 else range(2 * (r - 1), 2 * r)
+        if r == 0:
+            return (U, M)
+        if r == 1:
+            return range(N_TRACERS)
+        return range(2 * (r - 2), 2 * (r - 1))
 
     outgoing = ((0, north, has_north), (1, south, has_south), (2, east, None), (3, west, None))
     incoming = ((0, south, has_south), (1, north, has_north), (2, west, None), (3, east, None))
@@ -148,6 +153,7 @@
         each(r, outgoing, lambda c: c.wait_send())
 
     send(0)
+    send(1)
     receive(0)
 
     lane = lax.broadcasted_iota(jnp.int32, (KC, rows, cols), 2)
@@ -215,7 +221,7 @@
         def body(i, carry):
             k0 = pl.multiple_of(i * KC, KC)
             for f in (2 * g, 2 * g + 1):
-                b1[f, pl.ds(1 + k0, KC), inner, :] = step(b0, x0, f + 1, k0, g == 0)
+                b1[f, pl.ds(1 + k0, KC), inner, :] = step(b0, x0, f, k0, g == 0)
             return carry
 
         lax.fori_loop(0, levels // KC, body, 0)
@@ -229,17 +235,19 @@
 
         lax.fori_loop(0, levels // KC, body, 0)
 
+    receive(1)
     step1_loop(0)
-    send(1)
+    send(2)
     step1_loop(1)
-    send(2)
+    send(3)
     finish_sends(0)
-    receive(1)
+    finish_sends(1)
+    receive(2)
     step2_loop(0)
-    receive(2)
+    receive(3)
     step2_loop(1)
-    finish_sends(1)
     finish_sends(2)
+    finish_sends(3)
 
 
 def split_kernel(stacked, o_t, o_s, o_ct, o_cs, sem):
@@ -275,8 +283,8 @@
             pltpu.VMEM((20, levels, rows, cols), f32),
             pltpu.VMEM((levels + 1, rows, cols), f32),
             pltpu.SemaphoreType.DMA((6,)),
-            pltpu.SemaphoreType.DMA((3, 4)),
-            pltpu.SemaphoreType.DMA((3, 4)),
+            pltpu.SemaphoreType.DMA((4, 4)),
+            pltpu.SemaphoreType.DMA((4, 4)),
         ],
         compiler_params=pltpu.CompilerParams(
             collective_id=0, has_side_effects=True, vmem_limit_bytes=56 * 1024 * 1024

time: 32.7 us -> 31.5 us (0.963)
  Pallas kernels: 31.9 us -> 30.5 us
    pallas_call x1, Pallas kernels: 29.6 us -> 28.3 us  [local(): stacked = call(temp, salt, cot_temp, cot_salt, u_east, v_north, wet)]
where the time goes in v6:
time: 31.5 us; the launch traced here: 31.2 us
  Pallas kernels  30.5 us (97%)
  between operations  0.64 us (2%)
    pallas_call x1, Pallas kernels, local(): stacked = call(temp, salt, cot_temp, cot_salt, u_east, v_north, wet)  28.3 us
    pallas_call x1, Pallas kernels, local(): pl.pallas_call(split_kernel, out_shape=(out,) * 4, in_specs=[vmem_spec],...  2.22 us

profile of v6, /device:TPU:8, one launch (start us, length us, event | category | flops | bytes accessed | tf_op | source)
XLA Modules:
  0.0 31.2 jit_solution(16802200457735769698)
XLA Ops:
  0.6 28.3 %shard_map.102.stacked = f32[4,32,16,128]{3,2,1,0:T(8,128)} custom-call(f32[32,16,128]{2,1,0:T(8,128)} %t_hbm.1, f32[32,16,128]{2,1,0:T(8,128)} %s_hbm.1, f32[32,16,128]{2,1,0:T(8,128)} %ct_hbm.1, f32[32,16,128]{2,1,0:T(8,128)} %cs_hbm.1, f32[32,16,128]{2,1,0:T(8,128)} %u_hbm.1, f32[32,16,128]{2,1,0:T(8,128)} %v_hbm.1, s32[32,16,128]{2,1,0:T(8,128)} %wet_ref.1), custom_call_target="tpu_custom_call" | custom-call | tf_op jit(solution)/shard_map/pallas_call | solution.py:293
  28.9 2.2 %shard_map.103 = (f32[32,16,128]{2,1,0:T(8,128)}, f32[32,16,128]{2,1,0:T(8,128)}, f32[32,16,128]{2,1,0:T(8,128)}, f32[32,16,128]{2,1,0:T(8,128)}) custom-call(f32[4,32,16,128]{3,2,1,0:T(8,128)} %shard_map.102.stacked), custom_call_target="tpu_custom_call" | custom-call | tf_op jit(solution)/shard_map/pallas_call | solution.py:294

commit v7 on v6

--- a/solution.py
+++ b/solution.py
@@ -40,7 +40,7 @@
 def kernel(n_ew, n_ns, levels, rows, cols,
            t_hbm, s_hbm, ct_hbm, cs_hbm, u_hbm, v_hbm, wet_ref,
            o_all,
-           b0, x0, ts0, rt0, b1, x1, ts1, rt1, w, oz, load_sem, send_sem, recv_sem):
+           b0, x0, ts0, rt0, b1, x1, ts1, rt1, w, load_sem, send_sem, recv_sem):
     ew = lax.axis_index("ew")
     ns = lax.axis_index("ns")
     east = (lax.rem(ew + 1, n_ew), ns)
@@ -86,7 +86,6 @@
             buf[:, lev, pl.ds(PAD + rows, 2), :] = zr
 
     b0[M, lev, inner, :] = wet_ref[...].astype(jnp.float32)
-    oz[pl.ds(0, 1), :, :] = jnp.zeros((1, rows, cols), jnp.float32)
     for cp in loads:
         cp.wait()
 
@@ -172,21 +171,36 @@
         vm1, vm2, vp1 = rows_at(b0, V, k0, -1), rows_at(b0, V, k0, -2), rows_at(b0, V, k0, 1)
         nm2, nm1 = rows_at(b0, M, k0, -2), rows_at(b0, M, k0, -1)
         np1, np2 = rows_at(b0, M, k0, 1), rows_at(b0, M, k0, 2)
+        centre = None
         for base, (s_m2, s_m1, s_0, s_p1), (q_m2, q_m1, q_0, q_p1, q_p2) in (
             (0, (um2, um1, u0, up1), (mm2, mm1, m0, mp1, mp2)),
-            (10, (vm2, vm1, v0, vp1), (nm2, nm1, m0, np1, np2)),
+            (4, (vm2, vm1, v0, vp1), (nm2, nm1, m0, np1, np2)),
         ):
             a0 = coefficients(s_0)
             am1 = coefficients(s_m1)
             o0 = q_0 * q_p1
             om1 = q_m1 * q_0
-            for k in range(4):
-                w[base + k, kk] = o0 * a0[k]
-                w[base + 4 + k, kk] = om1 * am1[k]
-            w[base + 8, kk] = (q_p1 * q_p2) * coefficients(s_p1)[0]
-            w[base + 9, kk] = (q_m2 * q_m1) * coefficients(s_m2)[3]
+            here = [o0 * a0[k] for k in range(4)]
+            back = [om1 * am1[k] for k in range(4)]
+            ahead0 = (q_p1 * q_p2) * coefficients(s_p1)[0]
+            behind3 = (q_m2 * q_m1) * coefficients(s_m2)[3]
+            w[base + 0, kk] = back[0]
+            w[base + 1, kk] = back[1] - here[0]
+            w[base + 2, kk] = back[3] - here[2]
+            w[base + 3, kk] = -here[3]
+            w[8 + base + 0, kk] = -behind3
+            w[8 + base + 1, kk] = behind3 - back[2]
+            w[8 + base + 2, kk] = here[1] - ahead0
+            w[8 + base + 3, kk] = ahead0
+            mid = back[2] - here[1]
+            centre = mid if centre is None else centre + mid
+        m_dn = b0[M, pl.ds(k0, KC), inner, :]
         m_up = b0[M, pl.ds(2 + k0, KC), inner, :]
-        oz[pl.ds(1 + k0, KC)] = vertical_mix * (m0 * m_up)
+        z_lo = vertical_mix * (m_dn * m0)
+        z_hi = vertical_mix * (m0 * m_up)
+        w[16, kk] = z_lo
+        w[17, kk] = z_hi
+        w[18, kk] = 1.0 + centre - (z_lo + z_hi)
         return carry
 
     lax.fori_loop(0, levels // KC, weights_body, 0)
@@ -199,23 +213,11 @@
         yp1, yp2 = rows_at(src, f, k0, 1), rows_at(src, f, k0, 2)
         zm = src[f, pl.ds(k0, KC), inner, :]
         zp = src[f, pl.ds(2 + k0, KC), inner, :]
-        oz_lo = oz[pl.ds(k0, KC)]
-        oz_hi = oz[pl.ds(1 + k0, KC)]
-        if forward:
-            fxr = w[0, kk] * cm1 + w[1, kk] * c + w[2, kk] * cp1 + w[3, kk] * cp2
-            fxl = w[4, kk] * cm2 + w[5, kk] * cm1 + w[6, kk] * c + w[7, kk] * cp1
-            fyr = w[10, kk] * ym1 + w[11, kk] * c + w[12, kk] * yp1 + w[13, kk] * yp2
-            fyl = w[14, kk] * ym2 + w[15, kk] * ym1 + w[16, kk] * c + w[17, kk] * yp1
-            gl = oz_lo * (zm - c)
-            gr = oz_hi * (c - zp)
-            return c + (((fxl - fxr) + (fyl - fyr)) + (gl - gr))
-        bx = (w[8, kk] * (cp2 - cp1) + w[1, kk] * (cp1 - c)
-              + w[6, kk] * (c - cm1) + w[9, kk] * (cm1 - cm2))
-        by = (w[18, kk] * (yp2 - yp1) + w[11, kk] * (yp1 - c)
-              + w[16, kk] * (c - ym1) + w[19, kk] * (ym1 - ym2))
-        bz = oz_hi * (zp - c) - oz_lo * (c - zm)
-        return c + bx + by + bz
-
+        o = 0 if forward else 8
+        sx = (w[o + 0, kk] * cm2 + w[o + 1, kk] * cm1) + (w[o + 2, kk] * cp1 + w[o + 3, kk] * cp2)
+        sy = (w[o + 4, kk] * ym2 + w[o + 5, kk] * ym1) + (w[o + 6, kk] * yp1 + w[o + 7, kk] * yp2)
+        sz = w[16, kk] * zm + w[17, kk] * zp
+        return (w[18, kk] * c + sz) + (sx + sy)
 
     def step1_loop(g):
         def body(i, carry):
@@ -280,8 +282,7 @@
             pltpu.VMEM((N_TRACERS, levels, rows, cols), f32),
             pltpu.VMEM((N_TRACERS, cols, levels * rows), f32),
             pltpu.VMEM((N_TRACERS, cols, levels * rows), f32),
-            pltpu.VMEM((20, levels, rows, cols), f32),
-            pltpu.VMEM((levels + 1, rows, cols), f32),
+            pltpu.VMEM((19, levels, rows, cols), f32),
             pltpu.SemaphoreType.DMA((6,)),
             pltpu.SemaphoreType.DMA((4, 4)),
             pltpu.SemaphoreType.DMA((4, 4)),

time: 31.5 us -> 31.1 us (0.987)
    pallas_call x1, Pallas kernels: 28.3 us -> 28 us  [local(): stacked = call(temp, salt, cot_temp, cot_salt, u_east, v_north, wet)]
where the time goes in v7:
time: 31.1 us; the launch traced here: 30.8 us
  Pallas kernels  30.2 us (97%)
  between operations  0.64 us (2%)
    pallas_call x1, Pallas kernels, local(): stacked = call(temp, salt, cot_temp, cot_salt, u_east, v_north, wet)  28 us
    pallas_call x1, Pallas kernels, local(): pl.pallas_call(split_kernel, out_shape=(out,) * 4, in_specs=[vmem_spec],...  2.22 us

profile of v7, /device:TPU:8, one launch (start us, length us, event | category | flops | bytes accessed | tf_op | source)
XLA Modules:
  0.0 30.8 jit_solution(6462222672204427923)
XLA Ops:
  0.6 28.0 %shard_map.102.stacked = f32[4,32,16,128]{3,2,1,0:T(8,128)} custom-call(f32[32,16,128]{2,1,0:T(8,128)} %t_hbm.1, f32[32,16,128]{2,1,0:T(8,128)} %s_hbm.1, f32[32,16,128]{2,1,0:T(8,128)} %ct_hbm.1, f32[32,16,128]{2,1,0:T(8,128)} %cs_hbm.1, f32[32,16,128]{2,1,0:T(8,128)} %u_hbm.1, f32[32,16,128]{2,1,0:T(8,128)} %v_hbm.1, s32[32,16,128]{2,1,0:T(8,128)} %wet_ref.1), custom_call_target="tpu_custom_call" | custom-call | tf_op jit(solution)/shard_map/pallas_call | solution.py:294
  28.6 2.2 %shard_map.103 = (f32[32,16,128]{2,1,0:T(8,128)}, f32[32,16,128]{2,1,0:T(8,128)}, f32[32,16,128]{2,1,0:T(8,128)}, f32[32,16,128]{2,1,0:T(8,128)}) custom-call(f32[4,32,16,128]{3,2,1,0:T(8,128)} %shard_map.102.stacked), custom_call_target="tpu_custom_call" | custom-call | tf_op jit(solution)/shard_map/pallas_call | solution.py:295

commit v8 on v7

--- a/solution.py
+++ b/solution.py
@@ -95,9 +95,10 @@
     def group(r):
         if r == 0:
             return b0, ts0, rt0, x0, pl.ds(M, 2), pl.ds(U, 2)
-        if r == 1:
-            return b0, ts0, rt0, x0, pl.ds(0, N_TRACERS), pl.ds(0, N_TRACERS)
-        g = pl.ds(2 * (r - 2), 2)
+        if r <= N_TRACERS:
+            g = pl.ds(r - 1, 1)
+            return b0, ts0, rt0, x0, g, g
+        g = pl.ds(r - 1 - N_TRACERS, 1)
         return b1, ts1, rt1, x1, g, g
 
     def edge_copy(r, d, dev):
@@ -122,9 +123,9 @@
     def x_fields(r):
         if r == 0:
             return (U, M)
-        if r == 1:
-            return range(N_TRACERS)
-        return range(2 * (r - 2), 2 * (r - 1))
+        if r <= N_TRACERS:
+            return (r - 1,)
+        return (r - 1 - N_TRACERS,)
 
     outgoing = ((0, north, has_north), (1, south, has_south), (2, east, None), (3, west, None))
     incoming = ((0, south, has_south), (1, north, has_north), (2, west, None), (3, east, None))
@@ -151,8 +152,8 @@
     def finish_sends(r):
         each(r, outgoing, lambda c: c.wait_send())
 
-    send(0)
-    send(1)
+    for r in range(1 + N_TRACERS):
+        send(r)
     receive(0)
 
     lane = lax.broadcasted_iota(jnp.int32, (KC, rows, cols), 2)
@@ -219,37 +220,33 @@
         sz = w[16, kk] * zm + w[17, kk] * zp
         return (w[18, kk] * c + sz) + (sx + sy)
 
-    def step1_loop(g):
+    def step1_loop(f):
         def body(i, carry):
             k0 = pl.multiple_of(i * KC, KC)
-            for f in (2 * g, 2 * g + 1):
-                b1[f, pl.ds(1 + k0, KC), inner, :] = step(b0, x0, f, k0, g == 0)
+            b1[f, pl.ds(1 + k0, KC), inner, :] = step(b0, x0, f, k0, f < 2)
             return carry
 
         lax.fori_loop(0, levels // KC, body, 0)
 
-    def step2_loop(g):
+    def step2_loop(f):
         def body(i, carry):
             k0 = pl.multiple_of(i * KC, KC)
-            for f in (2 * g, 2 * g + 1):
-                o_all[f, pl.ds(k0, KC)] = step(b1, x1, f, k0, g == 0)
+            o_all[f, pl.ds(k0, KC)] = step(b1, x1, f, k0, f < 2)
             return carry
 
         lax.fori_loop(0, levels // KC, body, 0)
 
-    receive(1)
-    step1_loop(0)
-    send(2)
-    step1_loop(1)
-    send(3)
-    finish_sends(0)
-    finish_sends(1)
-    receive(2)
-    step2_loop(0)
-    receive(3)
-    step2_loop(1)
-    finish_sends(2)
-    finish_sends(3)
+    for f in range(N_TRACERS):
+        receive(1 + f)
+        step1_loop(f)
+        send(1 + N_TRACERS + f)
+    for r in range(1 + N_TRACERS):
+        finish_sends(r)
+    for f in range(N_TRACERS):
+        receive(1 + N_TRACERS + f)
+        step2_loop(f)
+    for f in range(N_TRACERS):
+        finish_sends(1 + N_TRACERS + f)
 
 
 def split_kernel(stacked, o_t, o_s, o_ct, o_cs, sem):
@@ -284,8 +281,8 @@
             pltpu.VMEM((N_TRACERS, cols, levels * rows), f32),
             pltpu.VMEM((19, levels, rows, cols), f32),
             pltpu.SemaphoreType.DMA((6,)),
-            pltpu.SemaphoreType.DMA((4, 4)),
-            pltpu.SemaphoreType.DMA((4, 4)),
+            pltpu.SemaphoreType.DMA((1 + 2 * N_TRACERS, 4)),
+            pltpu.SemaphoreType.DMA((1 + 2 * N_TRACERS, 4)),
         ],
         compiler_params=pltpu.CompilerParams(
             collective_id=0, has_side_effects=True, vmem_limit_bytes=56 * 1024 * 1024

time: 31.1 us -> 34.3 us (1.10)
  the two profiles are of different devices: /device:TPU:8 before, /device:TPU:1 now
where the time goes in v8:
time: 34.3 us; the launch traced here: 34.1 us
  Pallas kernels  33.5 us (98%)
  between operations  0.64 us (2%)
    pallas_call x1, Pallas kernels, local(): stacked = call(temp, salt, cot_temp, cot_salt, u_east, v_north, wet)  31.3 us
    pallas_call x1, Pallas kernels, local(): pl.pallas_call(split_kernel, out_shape=(out,) * 4, in_specs=[vmem_spec],...  2.22 us

profile of v8, /device:TPU:1, one launch (start us, length us, event | category | flops | bytes accessed | tf_op | source)
XLA Modules:
  0.0 34.1 jit_solution(5849441650275888136)
XLA Ops:
  0.6 31.3 %shard_map.102.stacked = f32[4,32,16,128]{3,2,1,0:T(8,128)} custom-call(f32[32,16,128]{2,1,0:T(8,128)} %t_hbm.1, f32[32,16,128]{2,1,0:T(8,128)} %s_hbm.1, f32[32,16,128]{2,1,0:T(8,128)} %ct_hbm.1, f32[32,16,128]{2,1,0:T(8,128)} %cs_hbm.1, f32[32,16,128]{2,1,0:T(8,128)} %u_hbm.1, f32[32,16,128]{2,1,0:T(8,128)} %v_hbm.1, s32[32,16,128]{2,1,0:T(8,128)} %wet_ref.1), custom_call_target="tpu_custom_call" | custom-call | tf_op jit(solution)/shard_map/pallas_call | solution.py:291
  31.9 2.2 %shard_map.103 = (f32[32,16,128]{2,1,0:T(8,128)}, f32[32,16,128]{2,1,0:T(8,128)}, f32[32,16,128]{2,1,0:T(8,128)}, f32[32,16,128]{2,1,0:T(8,128)}) custom-call(f32[4,32,16,128]{3,2,1,0:T(8,128)} %shard_map.102.stacked), custom_call_target="tpu_custom_call" | custom-call | tf_op jit(solution)/shard_map/pallas_call | solution.py:292

commit v9 on v7

--- a/solution.py
+++ b/solution.py
@@ -136,11 +136,18 @@
             else:
                 pl.when(cond)(lambda d=d, dev=dev: action(edge_copy(r, d, dev)))
 
-    def send(r):
+    def send_rows(r):
+        each(r, outgoing[:2], lambda c: c.start())
+
+    def send_columns(r):
         buf, ts = group(r)[:2]
         for f in x_fields(r):
             ts[f] = buf[f, lev, inner, :].reshape(levels * rows, cols).T
-        each(r, outgoing, lambda c: c.start())
+        each(r, outgoing[2:], lambda c: c.start())
+
+    def send(r):
+        send_rows(r)
+        send_columns(r)
 
     def receive(r):
         rt, x = group(r)[2:4]
@@ -151,8 +158,10 @@
     def finish_sends(r):
         each(r, outgoing, lambda c: c.wait_send())
 
-    send(0)
-    send(1)
+    send_rows(0)
+    send_rows(1)
+    send_columns(0)
+    send_columns(1)
     receive(0)
 
     lane = lax.broadcasted_iota(jnp.int32, (KC, rows, cols), 2)

time: 31.1 us -> 31.1 us (level)
  no operation moved by 1% of the time
where the time goes in v9:
time: 31.1 us; the launch traced here: 30.9 us
  Pallas kernels  30.2 us (97%)
  between operations  0.64 us (2%)
    pallas_call x1, Pallas kernels, local(): stacked = call(temp, salt, cot_temp, cot_salt, u_east, v_north, wet)  28 us
    pallas_call x1, Pallas kernels, local(): pl.pallas_call(split_kernel, out_shape=(out,) * 4, in_specs=[vmem_spec],...  2.22 us

profile of v9, /device:TPU:8, one launch (start us, length us, event | category | flops | bytes accessed | tf_op | source)
XLA Modules:
  0.0 30.9 jit_solution(17410889135210871862)
XLA Ops:
  0.6 28.0 %shard_map.102.stacked = f32[4,32,16,128]{3,2,1,0:T(8,128)} custom-call(f32[32,16,128]{2,1,0:T(8,128)} %t_hbm.1, f32[32,16,128]{2,1,0:T(8,128)} %s_hbm.1, f32[32,16,128]{2,1,0:T(8,128)} %ct_hbm.1, f32[32,16,128]{2,1,0:T(8,128)} %cs_hbm.1, f32[32,16,128]{2,1,0:T(8,128)} %u_hbm.1, f32[32,16,128]{2,1,0:T(8,128)} %v_hbm.1, s32[32,16,128]{2,1,0:T(8,128)} %wet_ref.1), custom_call_target="tpu_custom_call" | custom-call | tf_op jit(solution)/shard_map/pallas_call | solution.py:303
  28.6 2.2 %shard_map.103 = (f32[32,16,128]{2,1,0:T(8,128)}, f32[32,16,128]{2,1,0:T(8,128)}, f32[32,16,128]{2,1,0:T(8,128)}, f32[32,16,128]{2,1,0:T(8,128)}) custom-call(f32[4,32,16,128]{3,2,1,0:T(8,128)} %shard_map.102.stacked), custom_call_target="tpu_custom_call" | custom-call | tf_op jit(solution)/shard_map/pallas_call | solution.py:304

commit v10 on v9

--- a/solution.py
+++ b/solution.py
@@ -304,7 +304,7 @@
     return pl.pallas_call(
         split_kernel,
         out_shape=(out,) * 4,
-        in_specs=[vmem_spec],
+        in_specs=[any_spec],
         out_specs=(any_spec,) * 4,
         scratch_shapes=[pltpu.SemaphoreType.DMA((4,))],
     )(stacked)

time: 31.1 us -> 61.7 us (1.98)
  Pallas kernels: 30.2 us -> 60.9 us
    pallas_call x1, Pallas kernels: 2.22 us -> 32.9 us  [local(): pl.pallas_call(split_kernel, out_shape=(out,) * 4, in_specs=[any_spec], o...]
where the time goes in v10:
time: 61.7 us; the launch traced here: 61.5 us
  Pallas kernels  60.9 us (99%)
  between operations  0.64 us (1%)
    pallas_call x1, Pallas kernels, local(): pl.pallas_call(split_kernel, out_shape=(out,) * 4, in_specs=[any_spec], o...  32.9 us
    pallas_call x1, Pallas kernels, local(): stacked = call(temp, salt, cot_temp, cot_salt, u_east, v_north, wet)  28 us

profile of v10, /device:TPU:8, one launch (start us, length us, event | category | flops | bytes accessed | tf_op | source)
XLA Modules:
  0.0 61.5 jit_solution(17529088578762251075)
XLA Ops:
  0.6 28.0 %shard_map.102.stacked = f32[4,32,16,128]{3,2,1,0:T(8,128)} custom-call(f32[32,16,128]{2,1,0:T(8,128)} %t_hbm.1, f32[32,16,128]{2,1,0:T(8,128)} %s_hbm.1, f32[32,16,128]{2,1,0:T(8,128)} %ct_hbm.1, f32[32,16,128]{2,1,0:T(8,128)} %cs_hbm.1, f32[32,16,128]{2,1,0:T(8,128)} %u_hbm.1, f32[32,16,128]{2,1,0:T(8,128)} %v_hbm.1, s32[32,16,128]{2,1,0:T(8,128)} %wet_ref.1), custom_call_target="tpu_custom_call" | custom-call | tf_op jit(solution)/shard_map/pallas_call | solution.py:303
  28.6 32.9 %shard_map.103 = (f32[32,16,128]{2,1,0:T(8,128)}, f32[32,16,128]{2,1,0:T(8,128)}, f32[32,16,128]{2,1,0:T(8,128)}, f32[32,16,128]{2,1,0:T(8,128)}) custom-call(f32[4,32,16,128]{3,2,1,0:T(8,128)} %shard_map.102.stacked), custom_call_target="tpu_custom_call" | custom-call | tf_op jit(solution)/shard_map/pallas_call | solution.py:304

commit v11 on v9

--- a/solution.py
+++ b/solution.py
@@ -11,7 +11,7 @@
 vertical_mix = 0.2
 
 PAD = 8
-KC = 2
+KC = 8
 N_FIELDS = 7
 X_FIELDS = 6
 N_TRACERS = 4

time: 31.1 us -> 28.6 us (0.920)
  Pallas kernels: 30.2 us -> 27.8 us
    pallas_call x1, Pallas kernels: 28 us -> 25.6 us  [local(): stacked = call(temp, salt, cot_temp, cot_salt, u_east, v_north, wet)]
where the time goes in v11:
time: 28.6 us; the launch traced here: 28.4 us
  Pallas kernels  27.8 us (97%)
  between operations  0.64 us (2%)
    pallas_call x1, Pallas kernels, local(): stacked = call(temp, salt, cot_temp, cot_salt, u_east, v_north, wet)  25.6 us
    pallas_call x1, Pallas kernels, local(): pl.pallas_call(split_kernel, out_shape=(out,) * 4, in_specs=[vmem_spec],...  2.22 us

profile of v11, /device:TPU:8, one launch (start us, length us, event | category | flops | bytes accessed | tf_op | source)
XLA Modules:
  0.0 28.4 jit_solution(13438223374310394598)
XLA Ops:
  0.6 25.6 %shard_map.102.stacked = f32[4,32,16,128]{3,2,1,0:T(8,128)} custom-call(f32[32,16,128]{2,1,0:T(8,128)} %t_hbm.1, f32[32,16,128]{2,1,0:T(8,128)} %s_hbm.1, f32[32,16,128]{2,1,0:T(8,128)} %ct_hbm.1, f32[32,16,128]{2,1,0:T(8,128)} %cs_hbm.1, f32[32,16,128]{2,1,0:T(8,128)} %u_hbm.1, f32[32,16,128]{2,1,0:T(8,128)} %v_hbm.1, s32[32,16,128]{2,1,0:T(8,128)} %wet_ref.1), custom_call_target="tpu_custom_call" | custom-call | tf_op jit(solution)/shard_map/pallas_call | solution.py:303
  26.2 2.2 %shard_map.103 = (f32[32,16,128]{2,1,0:T(8,128)}, f32[32,16,128]{2,1,0:T(8,128)}, f32[32,16,128]{2,1,0:T(8,128)}, f32[32,16,128]{2,1,0:T(8,128)}) custom-call(f32[4,32,16,128]{3,2,1,0:T(8,128)} %shard_map.102.stacked), custom_call_target="tpu_custom_call" | custom-call | tf_op jit(solution)/shard_map/pallas_call | solution.py:304

commit v12 on v11

--- a/solution.py
+++ b/solution.py
@@ -212,7 +212,7 @@
         w[18, kk] = 1.0 + centre - (z_lo + z_hi)
         return carry
 
-    lax.fori_loop(0, levels // KC, weights_body, 0)
+    lax.fori_loop(0, levels // KC, weights_body, 0, unroll=True)
 
     def step(src, xh, f, k0, forward):
         kk = pl.ds(k0, KC)
@@ -235,7 +235,7 @@
                 b1[f, pl.ds(1 + k0, KC), inner, :] = step(b0, x0, f, k0, g == 0)
             return carry
 
-        lax.fori_loop(0, levels // KC, body, 0)
+        lax.fori_loop(0, levels // KC, body, 0, unroll=True)
 
     def step2_loop(g):
         def body(i, carry):
@@ -244,7 +244,7 @@
                 o_all[f, pl.ds(k0, KC)] = step(b1, x1, f, k0, g == 0)
             return carry
 
-        lax.fori_loop(0, levels // KC, body, 0)
+        lax.fori_loop(0, levels // KC, body, 0, unroll=True)
 
     receive(1)
     step1_loop(0)

time: 28.6 us -> 27.8 us (0.972)
  Pallas kernels: 27.8 us -> 26.9 us
    pallas_call x1, Pallas kernels: 25.6 us -> 24.7 us  [local(): stacked = call(temp, salt, cot_temp, cot_salt, u_east, v_north, wet)]
where the time goes in v12:
time: 27.8 us; the launch traced here: 27.6 us
  Pallas kernels  26.9 us (97%)
  between operations  0.64 us (2%)
    pallas_call x1, Pallas kernels, local(): stacked = call(temp, salt, cot_temp, cot_salt, u_east, v_north, wet)  24.7 us
    pallas_call x1, Pallas kernels, local(): pl.pallas_call(split_kernel, out_shape=(out,) * 4, in_specs=[vmem_spec],...  2.22 us

profile of v12, /device:TPU:8, one launch (start us, length us, event | category | flops | bytes accessed | tf_op | source)
XLA Modules:
  0.0 27.6 jit_solution(9143020585860957979)
XLA Ops:
  0.6 24.7 %shard_map.102.stacked = f32[4,32,16,128]{3,2,1,0:T(8,128)} custom-call(f32[32,16,128]{2,1,0:T(8,128)} %t_hbm.1, f32[32,16,128]{2,1,0:T(8,128)} %s_hbm.1, f32[32,16,128]{2,1,0:T(8,128)} %ct_hbm.1, f32[32,16,128]{2,1,0:T(8,128)} %cs_hbm.1, f32[32,16,128]{2,1,0:T(8,128)} %u_hbm.1, f32[32,16,128]{2,1,0:T(8,128)} %v_hbm.1, s32[32,16,128]{2,1,0:T(8,128)} %wet_ref.1), custom_call_target="tpu_custom_call" | custom-call | tf_op jit(solution)/shard_map/pallas_call | solution.py:303
  25.4 2.2 %shard_map.103 = (f32[32,16,128]{2,1,0:T(8,128)}, f32[32,16,128]{2,1,0:T(8,128)}, f32[32,16,128]{2,1,0:T(8,128)}, f32[32,16,128]{2,1,0:T(8,128)}) custom-call(f32[4,32,16,128]{3,2,1,0:T(8,128)} %shard_map.102.stacked), custom_call_target="tpu_custom_call" | custom-call | tf_op jit(solution)/shard_map/pallas_call | solution.py:304

commit v13 on v12

--- a/solution.py
+++ b/solution.py
@@ -95,9 +95,9 @@
     def group(r):
         if r == 0:
             return b0, ts0, rt0, x0, pl.ds(M, 2), pl.ds(U, 2)
-        if r == 1:
-            return b0, ts0, rt0, x0, pl.ds(0, N_TRACERS), pl.ds(0, N_TRACERS)
-        g = pl.ds(2 * (r - 2), 2)
+        g = pl.ds(2 * ((r - 1) % 2), 2)
+        if r <= 2:
+            return b0, ts0, rt0, x0, g, g
         return b1, ts1, rt1, x1, g, g
 
     def edge_copy(r, d, dev):
@@ -122,9 +122,8 @@
     def x_fields(r):
         if r == 0:
             return (U, M)
-        if r == 1:
-            return range(N_TRACERS)
-        return range(2 * (r - 2), 2 * (r - 1))
+        g = (r - 1) % 2
+        return range(2 * g, 2 * g + 2)
 
     outgoing = ((0, north, has_north), (1, south, has_south), (2, east, None), (3, west, None))
     incoming = ((0, south, has_south), (1, north, has_north), (2, west, None), (3, east, None))
@@ -158,10 +157,10 @@
     def finish_sends(r):
         each(r, outgoing, lambda c: c.wait_send())
 
-    send_rows(0)
-    send_rows(1)
-    send_columns(0)
-    send_columns(1)
+    for r in range(3):
+        send_rows(r)
+    for r in range(3):
+        send_columns(r)
     receive(0)
 
     lane = lax.broadcasted_iota(jnp.int32, (KC, rows, cols), 2)
@@ -248,17 +247,18 @@
 
     receive(1)
     step1_loop(0)
-    send(2)
+    send(3)
+    receive(2)
     step1_loop(1)
-    send(3)
-    finish_sends(0)
-    finish_sends(1)
-    receive(2)
+    send(4)
+    for r in range(3):
+        finish_sends(r)
+    receive(3)
     step2_loop(0)
-    receive(3)
+    receive(4)
     step2_loop(1)
-    finish_sends(2)
     finish_sends(3)
+    finish_sends(4)
 
 
 def split_kernel(stacked, o_t, o_s, o_ct, o_cs, sem):
@@ -293,8 +293,8 @@
             pltpu.VMEM((N_TRACERS, cols, levels * rows), f32),
             pltpu.VMEM((19, levels, rows, cols), f32),
             pltpu.SemaphoreType.DMA((6,)),
-            pltpu.SemaphoreType.DMA((4, 4)),
-            pltpu.SemaphoreType.DMA((4, 4)),
+            pltpu.SemaphoreType.DMA((5, 4)),
+            pltpu.SemaphoreType.DMA((5, 4)),
         ],
         compiler_params=pltpu.CompilerParams(
             collective_id=0, has_side_effects=True, vmem_limit_bytes=56 * 1024 * 1024

time: 27.8 us -> 27.8 us (level)
  no operation moved by 1% of the time
where the time goes in v13:
time: 27.8 us; the launch traced here: 27.6 us
  Pallas kernels  26.9 us (97%)
  between operations  0.64 us (2%)
    pallas_call x1, Pallas kernels, local(): stacked = call(temp, salt, cot_temp, cot_salt, u_east, v_north, wet)  24.7 us
    pallas_call x1, Pallas kernels, local(): pl.pallas_call(split_kernel, out_shape=(out,) * 4, in_specs=[vmem_spec],...  2.22 us

profile of v13, /device:TPU:8, one launch (start us, length us, event | category | flops | bytes accessed | tf_op | source)
XLA Modules:
  0.0 27.6 jit_solution(16981649457060627666)
XLA Ops:
  0.6 24.7 %shard_map.102.stacked = f32[4,32,16,128]{3,2,1,0:T(8,128)} custom-call(f32[32,16,128]{2,1,0:T(8,128)} %t_hbm.1, f32[32,16,128]{2,1,0:T(8,128)} %s_hbm.1, f32[32,16,128]{2,1,0:T(8,128)} %ct_hbm.1, f32[32,16,128]{2,1,0:T(8,128)} %cs_hbm.1, f32[32,16,128]{2,1,0:T(8,128)} %u_hbm.1, f32[32,16,128]{2,1,0:T(8,128)} %v_hbm.1, s32[32,16,128]{2,1,0:T(8,128)} %wet_ref.1), custom_call_target="tpu_custom_call" | custom-call | tf_op jit(solution)/shard_map/pallas_call | solution.py:303
  25.4 2.2 %shard_map.103 = (f32[32,16,128]{2,1,0:T(8,128)}, f32[32,16,128]{2,1,0:T(8,128)}, f32[32,16,128]{2,1,0:T(8,128)}, f32[32,16,128]{2,1,0:T(8,128)}) custom-call(f32[4,32,16,128]{3,2,1,0:T(8,128)} %shard_map.102.stacked), custom_call_target="tpu_custom_call" | custom-call | tf_op jit(solution)/shard_map/pallas_call | solution.py:304

commit v14 on v13

--- a/solution.py
+++ b/solution.py
@@ -40,7 +40,7 @@
 def kernel(n_ew, n_ns, levels, rows, cols,
            t_hbm, s_hbm, ct_hbm, cs_hbm, u_hbm, v_hbm, wet_ref,
            o_all,
-           b0, x0, ts0, rt0, b1, x1, ts1, rt1, w, load_sem, send_sem, recv_sem):
+           b0, x0, ts0, rt0, b1, x1, ts1, rt1, w, res, load_sem, send_sem, recv_sem, out_sem):
     ew = lax.axis_index("ew")
     ns = lax.axis_index("ns")
     east = (lax.rem(ew + 1, n_ew), ns)
@@ -240,7 +240,7 @@
         def body(i, carry):
             k0 = pl.multiple_of(i * KC, KC)
             for f in (2 * g, 2 * g + 1):
-                o_all[f, pl.ds(k0, KC)] = step(b1, x1, f, k0, g == 0)
+                res[f, pl.ds(k0, KC)] = step(b1, x1, f, k0, g == 0)
             return carry
 
         lax.fori_loop(0, levels // KC, body, 0, unroll=True)
@@ -253,21 +253,39 @@
     send(4)
     for r in range(3):
         finish_sends(r)
+    def store(g):
+        copies = []
+        for f in (2 * g, 2 * g + 1):
+            cp = pltpu.make_async_copy(res.at[f], o_all.at[f], out_sem.at[f])
+            cp.start()
+            copies.append(cp)
+        return copies
+
     receive(3)
     step2_loop(0)
+    stored = store(0)
     receive(4)
     step2_loop(1)
+    stored += store(1)
     finish_sends(3)
     finish_sends(4)
-
-
-def split_kernel(stacked, o_t, o_s, o_ct, o_cs, sem):
-    copies = []
+    for cp in stored:
+        cp.wait()
+
+
+def split_kernel(stacked, o_t, o_s, o_ct, o_cs, held, in_sem, out_sem):
+    ins = []
+    for f in range(N_TRACERS):
+        cp = pltpu.make_async_copy(stacked.at[f], held.at[f], in_sem.at[f])
+        cp.start()
+        ins.append(cp)
+    outs = []
     for f, dst in enumerate((o_t, o_s, o_ct, o_cs)):
-        cp = pltpu.make_async_copy(stacked.at[f], dst, sem.at[f])
+        ins[f].wait()
+        cp = pltpu.make_async_copy(held.at[f], dst, out_sem.at[f])
         cp.start()
-        copies.append(cp)
-    for cp in copies:
+        outs.append(cp)
+    for cp in outs:
         cp.wait()
 
 
@@ -281,7 +299,7 @@
         functools.partial(kernel, n_ew, n_ns, levels, rows, cols),
         out_shape=jax.ShapeDtypeStruct((N_TRACERS, levels, rows, cols), f32),
         in_specs=[any_spec] * 6 + [vmem_spec],
-        out_specs=vmem_spec,
+        out_specs=any_spec,
         scratch_shapes=[
             pltpu.VMEM((N_FIELDS, levels + 2, rows + 2 * PAD, cols), f32),
             pltpu.VMEM((X_FIELDS, levels, rows, cols), f32),
@@ -292,9 +310,11 @@
             pltpu.VMEM((N_TRACERS, cols, levels * rows), f32),
             pltpu.VMEM((N_TRACERS, cols, levels * rows), f32),
             pltpu.VMEM((19, levels, rows, cols), f32),
+            pltpu.VMEM((N_TRACERS, levels, rows, cols), f32),
             pltpu.SemaphoreType.DMA((6,)),
             pltpu.SemaphoreType.DMA((5, 4)),
             pltpu.SemaphoreType.DMA((5, 4)),
+            pltpu.SemaphoreType.DMA((N_TRACERS,)),
         ],
         compiler_params=pltpu.CompilerParams(
             collective_id=0, has_side_effects=True, vmem_limit_bytes=56 * 1024 * 1024
@@ -304,9 +324,13 @@
     return pl.pallas_call(
         split_kernel,
         out_shape=(out,) * 4,
-        in_specs=[vmem_spec],
+        in_specs=[any_spec],
         out_specs=(any_spec,) * 4,
-        scratch_shapes=[pltpu.SemaphoreType.DMA((4,))],
+        scratch_shapes=[
+            pltpu.VMEM((N_TRACERS, levels, rows, cols), f32),
+            pltpu.SemaphoreType.DMA((N_TRACERS,)),
+            pltpu.SemaphoreType.DMA((N_TRACERS,)),
+        ],
     )(stacked)
 
 

time: 27.8 us -> 27.3 us (0.982)
  Pallas kernels: 26.9 us -> 26.5 us
where the time goes in v14:
time: 27.3 us; the launch traced here: 27.2 us
  Pallas kernels  26.5 us (97%)
  between operations  0.64 us (2%)
    pallas_call x1, Pallas kernels, local(): stacked = call(temp, salt, cot_temp, cot_salt, u_east, v_north, wet)  24.6 us
    pallas_call x1, Pallas kernels, local(): pl.pallas_call(split_kernel, out_shape=(out,) * 4, in_specs=[any_spec], o...  1.98 us

profile of v14, /device:TPU:8, one launch (start us, length us, event | category | flops | bytes accessed | tf_op | source)
XLA Modules:
  0.0 27.2 jit_solution(6544447001018099705)
XLA Ops:
  0.6 24.6 %shard_map.102.stacked = f32[4,32,16,128]{3,2,1,0:T(8,128)} custom-call(f32[32,16,128]{2,1,0:T(8,128)} %t_hbm.1, f32[32,16,128]{2,1,0:T(8,128)} %s_hbm.1, f32[32,16,128]{2,1,0:T(8,128)} %ct_hbm.1, f32[32,16,128]{2,1,0:T(8,128)} %cs_hbm.1, f32[32,16,128]{2,1,0:T(8,128)} %u_hbm.1, f32[32,16,128]{2,1,0:T(8,128)} %v_hbm.1, s32[32,16,128]{2,1,0:T(8,128)} %wet_ref.1), custom_call_target="tpu_custom_call" | custom-call | tf_op jit(solution)/shard_map/pallas_call | solution.py:323
  25.2 2.0 %shard_map.103 = (f32[32,16,128]{2,1,0:T(8,128)}, f32[32,16,128]{2,1,0:T(8,128)}, f32[32,16,128]{2,1,0:T(8,128)}, f32[32,16,128]{2,1,0:T(8,128)}) custom-call(f32[4,32,16,128]{3,2,1,0:T(8,128)} %shard_map.102.stacked), custom_call_target="tpu_custom_call" | custom-call | tf_op jit(solution)/shard_map/pallas_call | solution.py:324

commit v15 on v14

--- a/solution.py
+++ b/solution.py
@@ -40,7 +40,7 @@
 def kernel(n_ew, n_ns, levels, rows, cols,
            t_hbm, s_hbm, ct_hbm, cs_hbm, u_hbm, v_hbm, wet_ref,
            o_all,
-           b0, x0, ts0, rt0, b1, x1, ts1, rt1, w, res, load_sem, send_sem, recv_sem, out_sem):
+           b0, x0, ts0, rt0, b1, x1, ts1, rt1, w, res, wet_vmem, load_sem, send_sem, recv_sem, out_sem):
     ew = lax.axis_index("ew")
     ns = lax.axis_index("ns")
     east = (lax.rem(ew + 1, n_ew), ns)
@@ -70,6 +70,8 @@
         cp = pltpu.make_async_copy(src, b0.at[f, lev, inner, :], load_sem.at[j])
         cp.start()
         loads.append(cp)
+    wet_load = pltpu.make_async_copy(wet_ref, wet_vmem, load_sem.at[len(fields)])
+    wet_load.start()
 
     for buf, nf in ((b0, N_FIELDS), (b1, N_TRACERS)):
         zl = jnp.zeros((nf, 1, rows + 2 * PAD, cols), jnp.float32)
@@ -85,7 +87,8 @@
         def _():
             buf[:, lev, pl.ds(PAD + rows, 2), :] = zr
 
-    b0[M, lev, inner, :] = wet_ref[...].astype(jnp.float32)
+    wet_load.wait()
+    b0[M, lev, inner, :] = wet_vmem[...].astype(jnp.float32)
     for cp in loads:
         cp.wait()
 
@@ -298,7 +301,7 @@
     call = pl.pallas_call(
         functools.partial(kernel, n_ew, n_ns, levels, rows, cols),
         out_shape=jax.ShapeDtypeStruct((N_TRACERS, levels, rows, cols), f32),
-        in_specs=[any_spec] * 6 + [vmem_spec],
+        in_specs=[any_spec] * 7,
         out_specs=any_spec,
         scratch_shapes=[
             pltpu.VMEM((N_FIELDS, levels + 2, rows + 2 * PAD, cols), f32),
@@ -311,7 +314,8 @@
             pltpu.VMEM((N_TRACERS, cols, levels * rows), f32),
             pltpu.VMEM((19, levels, rows, cols), f32),
             pltpu.VMEM((N_TRACERS, levels, rows, cols), f32),
-            pltpu.SemaphoreType.DMA((6,)),
+            pltpu.VMEM((levels, rows, cols), jnp.int32),
+            pltpu.SemaphoreType.DMA((7,)),
             pltpu.SemaphoreType.DMA((5, 4)),
             pltpu.SemaphoreType.DMA((5, 4)),
             pltpu.SemaphoreType.DMA((N_TRACERS,)),

time: 27.3 us -> 26.4 us (0.967)
  Pallas kernels: 26.5 us -> 25.6 us
    pallas_call x1, Pallas kernels: 24.6 us -> 23.7 us  [local(): stacked = call(temp, salt, cot_temp, cot_salt, u_east, v_north, wet)]
where the time goes in v15:
time: 26.4 us; the launch traced here: 26.3 us
  Pallas kernels  25.6 us (97%)
  between operations  0.64 us (2%)
    pallas_call x1, Pallas kernels, local(): stacked = call(temp, salt, cot_temp, cot_salt, u_east, v_north, wet)  23.7 us
    pallas_call x1, Pallas kernels, local(): pl.pallas_call(split_kernel, out_shape=(out,) * 4, in_specs=[any_spec], o...  1.98 us

profile of v15, /device:TPU:8, one launch (start us, length us, event | category | flops | bytes accessed | tf_op | source)
XLA Modules:
  0.0 26.3 jit_solution(14579568096538931059)
XLA Ops:
  0.6 23.7 %shard_map.102.stacked = f32[4,32,16,128]{3,2,1,0:T(8,128)} custom-call(f32[32,16,128]{2,1,0:T(8,128)} %t_hbm.1, f32[32,16,128]{2,1,0:T(8,128)} %s_hbm.1, f32[32,16,128]{2,1,0:T(8,128)} %ct_hbm.1, f32[32,16,128]{2,1,0:T(8,128)} %cs_hbm.1, f32[32,16,128]{2,1,0:T(8,128)} %u_hbm.1, f32[32,16,128]{2,1,0:T(8,128)} %v_hbm.1, s32[32,16,128]{2,1,0:T(8,128)} %wet_ref.1), custom_call_target="tpu_custom_call" | custom-call | tf_op jit(solution)/shard_map/pallas_call | solution.py:327
  24.3 2.0 %shard_map.103 = (f32[32,16,128]{2,1,0:T(8,128)}, f32[32,16,128]{2,1,0:T(8,128)}, f32[32,16,128]{2,1,0:T(8,128)}, f32[32,16,128]{2,1,0:T(8,128)}) custom-call(f32[4,32,16,128]{3,2,1,0:T(8,128)} %shard_map.102.stacked), custom_call_target="tpu_custom_call" | custom-call | tf_op jit(solution)/shard_map/pallas_call | solution.py:328

commit v16 on v15

--- a/solution.py
+++ b/solution.py
@@ -239,11 +239,16 @@
 
         lax.fori_loop(0, levels // KC, body, 0, unroll=True)
 
+    def out_copy(f, i):
+        chunk = pl.ds(pl.multiple_of(i * KC, KC), KC)
+        return pltpu.make_async_copy(res.at[f, chunk], o_all.at[f, chunk], out_sem.at[f, i])
+
     def step2_loop(g):
         def body(i, carry):
             k0 = pl.multiple_of(i * KC, KC)
             for f in (2 * g, 2 * g + 1):
                 res[f, pl.ds(k0, KC)] = step(b1, x1, f, k0, g == 0)
+                out_copy(f, i).start()
             return carry
 
         lax.fori_loop(0, levels // KC, body, 0, unroll=True)
@@ -256,24 +261,15 @@
     send(4)
     for r in range(3):
         finish_sends(r)
-    def store(g):
-        copies = []
-        for f in (2 * g, 2 * g + 1):
-            cp = pltpu.make_async_copy(res.at[f], o_all.at[f], out_sem.at[f])
-            cp.start()
-            copies.append(cp)
-        return copies
-
     receive(3)
     step2_loop(0)
-    stored = store(0)
     receive(4)
     step2_loop(1)
-    stored += store(1)
     finish_sends(3)
     finish_sends(4)
-    for cp in stored:
-        cp.wait()
+    for f in range(N_TRACERS):
+        for i in range(levels // KC):
+            out_copy(f, i).wait()
 
 
 def split_kernel(stacked, o_t, o_s, o_ct, o_cs, held, in_sem, out_sem):
@@ -318,7 +314,7 @@
             pltpu.SemaphoreType.DMA((7,)),
             pltpu.SemaphoreType.DMA((5, 4)),
             pltpu.SemaphoreType.DMA((5, 4)),
-            pltpu.SemaphoreType.DMA((N_TRACERS,)),
+            pltpu.SemaphoreType.DMA((N_TRACERS, levels // KC)),
         ],
         compiler_params=pltpu.CompilerParams(
             collective_id=0, has_side_effects=True, vmem_limit_bytes=56 * 1024 * 1024

time: 26.4 us -> 26.4 us (level)
  no operation moved by 1% of the time
where the time goes in v16:
time: 26.4 us; the launch traced here: 26.2 us
  Pallas kernels  25.6 us (97%)
  between operations  0.64 us (2%)
    pallas_call x1, Pallas kernels, local(): stacked = call(temp, salt, cot_temp, cot_salt, u_east, v_north, wet)  23.6 us
    pallas_call x1, Pallas kernels, local(): pl.pallas_call(split_kernel, out_shape=(out,) * 4, in_specs=[any_spec], o...  1.98 us

profile of v16, /device:TPU:8, one launch (start us, length us, event | category | flops | bytes accessed | tf_op | source)
XLA Modules:
  0.0 26.2 jit_solution(4137993572358047244)
XLA Ops:
  0.6 23.6 %shard_map.102.stacked = f32[4,32,16,128]{3,2,1,0:T(8,128)} custom-call(f32[32,16,128]{2,1,0:T(8,128)} %t_hbm.1, f32[32,16,128]{2,1,0:T(8,128)} %s_hbm.1, f32[32,16,128]{2,1,0:T(8,128)} %ct_hbm.1, f32[32,16,128]{2,1,0:T(8,128)} %cs_hbm.1, f32[32,16,128]{2,1,0:T(8,128)} %u_hbm.1, f32[32,16,128]{2,1,0:T(8,128)} %v_hbm.1, s32[32,16,128]{2,1,0:T(8,128)} %wet_ref.1), custom_call_target="tpu_custom_call" | custom-call | tf_op jit(solution)/shard_map/pallas_call | solution.py:323
  24.2 2.0 %shard_map.103 = (f32[32,16,128]{2,1,0:T(8,128)}, f32[32,16,128]{2,1,0:T(8,128)}, f32[32,16,128]{2,1,0:T(8,128)}, f32[32,16,128]{2,1,0:T(8,128)}) custom-call(f32[4,32,16,128]{3,2,1,0:T(8,128)} %shard_map.102.stacked), custom_call_target="tpu_custom_call" | custom-call | tf_op jit(solution)/shard_map/pallas_call | solution.py:324

commit v17 on v16

--- a/solution.py
+++ b/solution.py
@@ -273,15 +273,18 @@
 
 
 def split_kernel(stacked, o_t, o_s, o_ct, o_cs, held, in_sem, out_sem):
+    levels = stacked.shape[1]
+    chunks = [(f, pl.ds(i * KC, KC)) for f in range(N_TRACERS) for i in range(levels // KC)]
     ins = []
-    for f in range(N_TRACERS):
-        cp = pltpu.make_async_copy(stacked.at[f], held.at[f], in_sem.at[f])
+    for j, (f, kk) in enumerate(chunks):
+        cp = pltpu.make_async_copy(stacked.at[f, kk], held.at[f, kk], in_sem.at[j])
         cp.start()
         ins.append(cp)
+    dsts = (o_t, o_s, o_ct, o_cs)
     outs = []
-    for f, dst in enumerate((o_t, o_s, o_ct, o_cs)):
-        ins[f].wait()
-        cp = pltpu.make_async_copy(held.at[f], dst, out_sem.at[f])
+    for j, (f, kk) in enumerate(chunks):
+        ins[j].wait()
+        cp = pltpu.make_async_copy(held.at[f, kk], dsts[f].at[kk], out_sem.at[j])
         cp.start()
         outs.append(cp)
     for cp in outs:
@@ -328,8 +331,8 @@
         out_specs=(any_spec,) * 4,
         scratch_shapes=[
             pltpu.VMEM((N_TRACERS, levels, rows, cols), f32),
-            pltpu.SemaphoreType.DMA((N_TRACERS,)),
-            pltpu.SemaphoreType.DMA((N_TRACERS,)),
+            pltpu.SemaphoreType.DMA((N_TRACERS * levels // KC,)),
+            pltpu.SemaphoreType.DMA((N_TRACERS * levels // KC,)),
         ],
     )(stacked)
 

time: 26.4 us -> 26.6 us (level)
  no operation moved by 1% of the time
where the time goes in v17:
time: 26.6 us; the launch traced here: 26.4 us
  Pallas kernels  25.8 us (97%)
  between operations  0.64 us (2%)
    pallas_call x1, Pallas kernels, local(): stacked = call(temp, salt, cot_temp, cot_salt, u_east, v_north, wet)  23.6 us
    pallas_call x1, Pallas kernels, local(): pl.pallas_call(split_kernel, out_shape=(out,) * 4, in_specs=[any_spec], o...  2.16 us

profile of v17, /device:TPU:8, one launch (start us, length us, event | category | flops | bytes accessed | tf_op | source)
XLA Modules:
  0.0 26.4 jit_solution(13075362285828766735)
XLA Ops:
  0.6 23.6 %shard_map.102.stacked = f32[4,32,16,128]{3,2,1,0:T(8,128)} custom-call(f32[32,16,128]{2,1,0:T(8,128)} %t_hbm.1, f32[32,16,128]{2,1,0:T(8,128)} %s_hbm.1, f32[32,16,128]{2,1,0:T(8,128)} %ct_hbm.1, f32[32,16,128]{2,1,0:T(8,128)} %cs_hbm.1, f32[32,16,128]{2,1,0:T(8,128)} %u_hbm.1, f32[32,16,128]{2,1,0:T(8,128)} %v_hbm.1, s32[32,16,128]{2,1,0:T(8,128)} %wet_ref.1), custom_call_target="tpu_custom_call" | custom-call | tf_op jit(solution)/shard_map/pallas_call | solution.py:326
  24.2 2.2 %shard_map.103 = (f32[32,16,128]{2,1,0:T(8,128)}, f32[32,16,128]{2,1,0:T(8,128)}, f32[32,16,128]{2,1,0:T(8,128)}, f32[32,16,128]{2,1,0:T(8,128)}) custom-call(f32[4,32,16,128]{3,2,1,0:T(8,128)} %shard_map.102.stacked), custom_call_target="tpu_custom_call" | custom-call | tf_op jit(solution)/shard_map/pallas_call | solution.py:327

commit v18 on v16

--- a/solution.py
+++ b/solution.py
@@ -11,7 +11,7 @@
 vertical_mix = 0.2
 
 PAD = 8
-KC = 8
+KC = 4
 N_FIELDS = 7
 X_FIELDS = 6
 N_TRACERS = 4

time: 26.4 us -> 26.3 us (level)
  no operation moved by 1% of the time
where the time goes in v18:
time: 26.3 us; the launch traced here: 26.1 us
  Pallas kernels  25.5 us (97%)
  between operations  0.64 us (2%)
    pallas_call x1, Pallas kernels, local(): stacked = call(temp, salt, cot_temp, cot_salt, u_east, v_north, wet)  23.5 us
    pallas_call x1, Pallas kernels, local(): pl.pallas_call(split_kernel, out_shape=(out,) * 4, in_specs=[any_spec], o...  1.98 us

profile of v18, /device:TPU:8, one launch (start us, length us, event | category | flops | bytes accessed | tf_op | source)
XLA Modules:
  0.0 26.1 jit_solution(5215014449530456649)
XLA Ops:
  0.6 23.5 %shard_map.102.stacked = f32[4,32,16,128]{3,2,1,0:T(8,128)} custom-call(f32[32,16,128]{2,1,0:T(8,128)} %t_hbm.1, f32[32,16,128]{2,1,0:T(8,128)} %s_hbm.1, f32[32,16,128]{2,1,0:T(8,128)} %ct_hbm.1, f32[32,16,128]{2,1,0:T(8,128)} %cs_hbm.1, f32[32,16,128]{2,1,0:T(8,128)} %u_hbm.1, f32[32,16,128]{2,1,0:T(8,128)} %v_hbm.1, s32[32,16,128]{2,1,0:T(8,128)} %wet_ref.1), custom_call_target="tpu_custom_call" | custom-call | tf_op jit(solution)/shard_map/pallas_call | solution.py:323
  24.1 2.0 %shard_map.103 = (f32[32,16,128]{2,1,0:T(8,128)}, f32[32,16,128]{2,1,0:T(8,128)}, f32[32,16,128]{2,1,0:T(8,128)}, f32[32,16,128]{2,1,0:T(8,128)}) custom-call(f32[4,32,16,128]{3,2,1,0:T(8,128)} %shard_map.102.stacked), custom_call_target="tpu_custom_call" | custom-call | tf_op jit(solution)/shard_map/pallas_call | solution.py:324

commit v19 on v18

--- a/solution.py
+++ b/solution.py
@@ -160,9 +160,10 @@
     def finish_sends(r):
         each(r, outgoing, lambda c: c.wait_send())
 
-    for r in range(3):
+    send(0)
+    for r in (1, 2):
         send_rows(r)
-    for r in range(3):
+    for r in (1, 2):
         send_columns(r)
     receive(0)
 

time: 26.3 us -> 26.3 us (level)
  no operation moved by 1% of the time
where the time goes in v19:
time: 26.3 us; the launch traced here: 26.1 us
  Pallas kernels  25.5 us (97%)
  between operations  0.64 us (2%)
    pallas_call x1, Pallas kernels, local(): stacked = call(temp, salt, cot_temp, cot_salt, u_east, v_north, wet)  23.5 us
    pallas_call x1, Pallas kernels, local(): pl.pallas_call(split_kernel, out_shape=(out,) * 4, in_specs=[any_spec], o...  1.98 us

profile of v19, /device:TPU:8, one launch (start us, length us, event | category | flops | bytes accessed | tf_op | source)
XLA Modules:
  0.0 26.1 jit_solution(16795835555547596167)
XLA Ops:
  0.6 23.5 %shard_map.102.stacked = f32[4,32,16,128]{3,2,1,0:T(8,128)} custom-call(f32[32,16,128]{2,1,0:T(8,128)} %t_hbm.1, f32[32,16,128]{2,1,0:T(8,128)} %s_hbm.1, f32[32,16,128]{2,1,0:T(8,128)} %ct_hbm.1, f32[32,16,128]{2,1,0:T(8,128)} %cs_hbm.1, f32[32,16,128]{2,1,0:T(8,128)} %u_hbm.1, f32[32,16,128]{2,1,0:T(8,128)} %v_hbm.1, s32[32,16,128]{2,1,0:T(8,128)} %wet_ref.1), custom_call_target="tpu_custom_call" | custom-call | tf_op jit(solution)/shard_map/pallas_call | solution.py:324
  24.1 2.0 %shard_map.103 = (f32[32,16,128]{2,1,0:T(8,128)}, f32[32,16,128]{2,1,0:T(8,128)}, f32[32,16,128]{2,1,0:T(8,128)}, f32[32,16,128]{2,1,0:T(8,128)}) custom-call(f32[4,32,16,128]{3,2,1,0:T(8,128)} %shard_map.102.stacked), custom_call_target="tpu_custom_call" | custom-call | tf_op jit(solution)/shard_map/pallas_call | solution.py:325

commit v20 on v18

--- a/solution.py
+++ b/solution.py
@@ -11,7 +11,7 @@
 vertical_mix = 0.2
 
 PAD = 8
-KC = 4
+KC = 2
 N_FIELDS = 7
 X_FIELDS = 6
 N_TRACERS = 4

time: 26.3 us -> 26.1 us (level)
  no operation moved by 1% of the time
where the time goes in v20:
time: 26.1 us; the launch traced here: 25.9 us
  Pallas kernels  25.3 us (97%)
  between operations  0.64 us (2%)
    pallas_call x1, Pallas kernels, local(): stacked = call(temp, salt, cot_temp, cot_salt, u_east, v_north, wet)  23.3 us
    pallas_call x1, Pallas kernels, local(): pl.pallas_call(split_kernel, out_shape=(out,) * 4, in_specs=[any_spec], o...  1.98 us

profile of v20, /device:TPU:8, one launch (start us, length us, event | category | flops | bytes accessed | tf_op | source)
XLA Modules:
  0.0 25.9 jit_solution(8224155656103060095)
XLA Ops:
  0.6 23.3 %shard_map.102.stacked = f32[4,32,16,128]{3,2,1,0:T(8,128)} custom-call(f32[32,16,128]{2,1,0:T(8,128)} %t_hbm.1, f32[32,16,128]{2,1,0:T(8,128)} %s_hbm.1, f32[32,16,128]{2,1,0:T(8,128)} %ct_hbm.1, f32[32,16,128]{2,1,0:T(8,128)} %cs_hbm.1, f32[32,16,128]{2,1,0:T(8,128)} %u_hbm.1, f32[32,16,128]{2,1,0:T(8,128)} %v_hbm.1, s32[32,16,128]{2,1,0:T(8,128)} %wet_ref.1), custom_call_target="tpu_custom_call" | custom-call | tf_op jit(solution)/shard_map/pallas_call | solution.py:323
  24.0 2.0 %shard_map.103 = (f32[32,16,128]{2,1,0:T(8,128)}, f32[32,16,128]{2,1,0:T(8,128)}, f32[32,16,128]{2,1,0:T(8,128)}, f32[32,16,128]{2,1,0:T(8,128)}) custom-call(f32[4,32,16,128]{3,2,1,0:T(8,128)} %shard_map.102.stacked), custom_call_target="tpu_custom_call" | custom-call | tf_op jit(solution)/shard_map/pallas_call | solution.py:324
